TPU v7x, 128 devices: a whole 4x4x4 slice. The times are simulated.
128 devices in a mesh: shot: 8 (over x, core), beam: 16 (over z, y).
Axes of the slice: x: 4, y: 4, z: 4, core: 2. Of those that a mesh axis runs over, the one named last changes fastest.
Arguments:
- traces: bfloat16 [8, 4096, 128], P('shot', 'beam'), may hold values from -6 to 6
- send_table: int32 [8, 16, 16, 16], P('shot'), may hold values from 0 to 255
- window_slots: int32 [8, 128, 32], P('shot', 'beam'), may hold values from 0 to 255
- ray_depth: float32 [8, 4096, 32, 128], P('shot', 'beam'), may hold values from 0 to 0.25
- ray_lateral: float32 [4096, 32, 128], P('beam'), may hold values from 0 to 0.25
- ray_spread: float32 [4096, 32, 128], P('beam'), may hold values from 0.0001 to 0.004
- ray_index: int32 [128, 12], P('beam'), may hold values from 0 to 255
- foot_count: int32 [16, 8], P('beam'), may hold values from 1 to 12, 80 in all within a row
- foot_tiles: int32 [128, 12], replicated, may hold values from 0 to 511, as said below
- tile_owner: int32 [512], replicated, may hold values from 0 to 127, as said below
Outputs:
- image_tiles: float32 [512, 128, 128], P(('shot', 'beam'))
Inputs may be any that keep to these rules, and one draw needn't show every extreme that they name: `send_table`: entry [s, j, g, i] is a row among the traces of shot gather s held by beam index j. `window_slots`: a slot of the block that the centre's group received, numbered source by source. `ray_index`: a row within the ray table of the centre's group. `foot_count`: the 8 counts of each group sum to 80. `foot_tiles`: entries past a centre's count hold tiles too; one centre's entries have distinct owners; within one group, entries whose tiles have the same owner name the same tile. `tile_owner`: each owner holds exactly 4 tiles.
All inputs are finite; a program needn't handle non-finite values.
Results may differ from a plain program's by a relative error of at most 0.0048.
Values may be sent and summed in bfloat16 or wider, within the bound.
A program may use at most 192 MiB of HBM per device.

v0:
```python
import math

import jax
import jax.numpy as jnp
from jax import lax
from jax.sharding import PartitionSpec as P

FREQUENCIES = 64
DIRECTIONS = 32
WINDOW = 32


def slant_tables():
    freq_index = jnp.arange(FREQUENCIES, dtype=jnp.float32)
    angular = 2.0 * math.pi * (4.0 + 60.0 * freq_index / FREQUENCIES)
    centred = jnp.arange(WINDOW, dtype=jnp.float32) - 0.5 * (WINDOW - 1)
    taper_weight = jnp.exp(-((centred / (0.25 * WINDOW)) ** 2)) / math.sqrt(WINDOW)
    slowness = 2e-05 * (jnp.arange(DIRECTIONS, dtype=jnp.float32) - 0.5 * (DIRECTIONS - 1))
    stack_angle = angular[:, None, None] * slowness[None, :, None] * (25.0 * centred)[None, None, :]
    stack_real = (taper_weight * jnp.cos(stack_angle)).astype(jnp.bfloat16)
    stack_imag = (-taper_weight * jnp.sin(stack_angle)).astype(jnp.bfloat16)
    return (angular, stack_real, stack_imag)


def pair_factors(
    beam_real, beam_imag, depth_times, lateral_times, spread_rates, live_mask, angular
):
    direction_count = beam_real.shape[1]
    freq_count = beam_real.shape[2]
    pair_count = depth_times.shape[0]
    weight_scale = (live_mask / math.sqrt(direction_count * freq_count))[:, None, None, None]
    depth_phase = angular[None, None, :, None] * depth_times[:, :, None, :]
    depth_cos = jnp.cos(depth_phase)
    depth_sin = jnp.sin(depth_phase)
    part_real = (beam_real[..., None] * depth_cos - beam_imag[..., None] * depth_sin) * weight_scale
    part_imag = (beam_real[..., None] * depth_sin + beam_imag[..., None] * depth_cos) * weight_scale
    depth_factor = jnp.stack([part_real, -part_imag], axis=1).astype(jnp.bfloat16)
    lateral_phase = angular[None, None, :, None] * lateral_times[:, :, None, :]
    damping = jnp.exp(-angular[None, None, :, None] * spread_rates[:, :, None, :])
    lateral_factor = jnp.stack(
        [damping * jnp.cos(lateral_phase), damping * jnp.sin(lateral_phase)], axis=1
    ).astype(jnp.bfloat16)
    depth_factor = depth_factor.reshape(
        pair_count, 2 * direction_count * freq_count, depth_times.shape[2]
    )
    lateral_factor = lateral_factor.reshape(
        pair_count, 2 * direction_count * freq_count, lateral_times.shape[2]
    )
    return (depth_factor, lateral_factor)


def body(
    traces,
    send_table,
    window_slots,
    ray_depth,
    ray_lateral,
    ray_spread,
    ray_index,
    foot_count,
    foot_tiles,
    tile_owner,
):
    groups = lax.axis_size("beam")
    shot_count = lax.axis_size("shot")
    group_id = lax.axis_index("beam")
    owner_count = shot_count * groups
    angular, stack_real, stack_imag = slant_tables()
    trace_rows = traces[0]
    trace_dev = trace_rows.shape[0]
    routes = send_table[0]
    all_rows = lax.all_gather(trace_rows, "beam", axis=0, tiled=True)
    my_routes = lax.dynamic_index_in_dim(routes, group_id, 1, keepdims=False)
    flat_index = (jnp.arange(groups, dtype=jnp.int32)[:, None] * trace_dev + my_routes).reshape(-1)
    arrived = all_rows[flat_index]
    slot_table = window_slots[0]
    centre_count = slot_table.shape[0]
    window = slot_table.shape[1]
    windows = arrived[slot_table.reshape(-1)].reshape(centre_count, window, -1)
    freq_count = angular.shape[0]
    trace_real = windows[..., :freq_count]
    trace_imag = windows[..., freq_count:]
    beam_real = jnp.einsum(
        "fpk,ckf->cpf", stack_real, trace_real, preferred_element_type=jnp.float32
    ) - jnp.einsum("fpk,ckf->cpf", stack_imag, trace_imag, preferred_element_type=jnp.float32)
    beam_imag = jnp.einsum(
        "fpk,ckf->cpf", stack_real, trace_imag, preferred_element_type=jnp.float32
    ) + jnp.einsum("fpk,ckf->cpf", stack_imag, trace_real, preferred_element_type=jnp.float32)
    foot_slots = ray_index.shape[1]
    entries = centre_count * foot_slots
    entry_ids = jnp.arange(entries, dtype=jnp.int32)
    centre_local = entry_ids // foot_slots
    slot_local = entry_ids % foot_slots
    alive_flag = (slot_local < foot_count[0][centre_local]).astype(jnp.int32)
    ray_rows = ray_index.reshape(-1)
    my_tiles = lax.dynamic_slice_in_dim(
        foot_tiles, group_id * centre_count, centre_count, 0
    ).reshape(-1)
    entry_owner = tile_owner[my_tiles]
    depth_table = ray_depth[0]
    depth_cells = depth_table.shape[2]
    lateral_cells = ray_lateral.shape[2]

    def one_block(buffer, chosen):
        centres = centre_local[chosen]
        rows_now = ray_rows[chosen]
        depth_factor, lateral_factor = pair_factors(
            beam_real[centres],
            beam_imag[centres],
            depth_table[rows_now],
            ray_lateral[rows_now],
            ray_spread[rows_now],
            alive_flag[chosen].astype(jnp.float32),
            angular,
        )
        contribution = jnp.einsum(
            "brz,brx->bzx", depth_factor, lateral_factor, preferred_element_type=jnp.float32
        )
        return (buffer.at[entry_owner[chosen]].add(contribution), None)

    buffer_start = jnp.zeros((owner_count, depth_cells, lateral_cells), jnp.float32)
    buffer, _ = lax.scan(one_block, buffer_start, entry_ids.reshape(-1, 8))
    tile_count = tile_owner.shape[0]
    tiles_each = tile_count // owner_count
    tile_order = jnp.argsort(tile_owner, stable=True)
    tile_rank = (
        jnp.zeros((tile_count,), jnp.int32)
        .at[tile_order]
        .set(jnp.arange(tile_count, dtype=jnp.int32))
    )
    tile_slot = tile_rank % tiles_each
    slot_range = jnp.arange(tiles_each, dtype=jnp.int32)
    owner_range = jnp.arange(owner_count, dtype=jnp.int32)
    owner_slot = jnp.max(
        jnp.where(entry_owner[None, :] == owner_range[:, None], tile_slot[my_tiles][None, :], 0),
        axis=1,
    )
    placed = (owner_slot[:, None] == slot_range[None, :]).astype(jnp.float32)
    return lax.psum_scatter(
        (buffer[:, None] * placed[:, :, None, None]).reshape(
            tiles_each * lax.axis_size(("shot", "beam")), depth_cells, lateral_cells
        ),
        ("shot", "beam"),
        scatter_dimension=0,
        tiled=True,
    )


def solution(mesh):
    in_specs = (
        P("shot", "beam", None),
        P("shot", None, None, None),
        P("shot", "beam", None),
        P("shot", "beam", None, None),
        P("beam", None, None),
        P("beam", None, None),
        P("beam", None),
        P("beam", None),
        P(),
        P(),
    )
    out_specs = P(("shot", "beam"), None, None)
    return jax.shard_map(body, mesh=mesh, in_specs=in_specs, out_specs=out_specs, check_vma=False)
```

profile of v0, /device:TPU:1, one launch (start us, length us, event | category | flops | bytes accessed | tf_op | source)
XLA Modules:
  0.0 1888.4 jit_solution(14164145799963792283)
XLA Ops:
  22.5 31.1 %all-gather.3.cloned.1.call-done = bf16[1,4096,128]{2,1,0:T(8,128)(2,1)} async-done(((bf16[1,256,128]{2,1,0:T(8,128)(2,1)}), bf16[1,4096,128]{2,1,0:T(8,128)(2,1)}) %all-gather.3.cloned.1.call-update) | async-done | bytes 1048592 | tf_op jit(solution)/shard_map/all_gather | solution.py:72
  76.2 1117.0 %while.13 = (s32[]{:T(128)}, f32[128,128,128]{2,1,0:T(8,128)}, s32[12,8]{1,0:T(8,128)S(1)}, s32[96]{0:T(128)S(1)}, f32[8,32,64]{2,1,0:T(8,128)S(1)}, /*index=5*/...) while((s32[]{:T(128)}, f32[128,128,128]{2,1,0:T(8,128)}, ...), condition=%wide.region_2.3_spmd.clone.clone, body=%wide.region_0.2_spmd.clone.clone.sunk | while | flops 1120017792 | bytes 70794200 | solution.py:122
  82.1 4.9 compare_convert_fusion.2
  99.1 63.0 %fusion.83 = (bf16[8,1,32,64,128]{4,3,2,1,0:T(8,128)(2,1)S(1)}, bf16[8,1,32,64,128]{4,3,2,1,0:T(8,128)(2,1)S(1)}, bf16[8,1,32,64,128]{4,3,2,1,0:T(8,128)(2,1)S(1)}, bf16[8,1,32,64,128]{4,3,2,1,0:T(8,128)(2,1)S(1)}) fusion(f32[8,32,128]{2,1,0:T(8,128)S(1)} %gather_fusion.2, f32[8,32,128]{2,1,0:T(8,128)S(1)} %gather_fusion.3, ...), kind=kLoop, calls=%fused_computation.35.clone.1 | loop fusion | flops 37748736 | bytes 17302048 | tf_op jit(solution)/shard_map/convert
  166.1 5.9 fusion.84
  174.7 4.9 compare_convert_fusion.2
  191.7 63.0 %fusion.83 = (bf16[8,1,32,64,128]{4,3,2,1,0:T(8,128)(2,1)S(1)}, bf16[8,1,32,64,128]{4,3,2,1,0:T(8,128)(2,1)S(1)}, bf16[8,1,32,64,128]{4,3,2,1,0:T(8,128)(2,1)S(1)}, bf16[8,1,32,64,128]{4,3,2,1,0:T(8,128)(2,1)S(1)}) fusion(f32[8,32,128]{2,1,0:T(8,128)S(1)} %gather_fusion.2, f32[8,32,128]{2,1,0:T(8,128)S(1)} %gather_fusion.3, ...), kind=kLoop, calls=%fused_computation.35.clone.1 | loop fusion | flops 37748736 | bytes 17302048 | tf_op jit(solution)/shard_map/convert
  258.7 5.9 fusion.84
  267.3 4.9 compare_convert_fusion.2
  284.3 63.0 %fusion.83 = (bf16[8,1,32,64,128]{4,3,2,1,0:T(8,128)(2,1)S(1)}, bf16[8,1,32,64,128]{4,3,2,1,0:T(8,128)(2,1)S(1)}, bf16[8,1,32,64,128]{4,3,2,1,0:T(8,128)(2,1)S(1)}, bf16[8,1,32,64,128]{4,3,2,1,0:T(8,128)(2,1)S(1)}) fusion(f32[8,32,128]{2,1,0:T(8,128)S(1)} %gather_fusion.2, f32[8,32,128]{2,1,0:T(8,128)S(1)} %gather_fusion.3, ...), kind=kLoop, calls=%fused_computation.35.clone.1 | loop fusion | flops 37748736 | bytes 17302048 | tf_op jit(solution)/shard_map/convert
  351.3 5.9 fusion.84
  359.9 4.9 compare_convert_fusion.2
  376.9 63.0 %fusion.83 = (bf16[8,1,32,64,128]{4,3,2,1,0:T(8,128)(2,1)S(1)}, bf16[8,1,32,64,128]{4,3,2,1,0:T(8,128)(2,1)S(1)}, bf16[8,1,32,64,128]{4,3,2,1,0:T(8,128)(2,1)S(1)}, bf16[8,1,32,64,128]{4,3,2,1,0:T(8,128)(2,1)S(1)}) fusion(f32[8,32,128]{2,1,0:T(8,128)S(1)} %gather_fusion.2, f32[8,32,128]{2,1,0:T(8,128)S(1)} %gather_fusion.3, ...), kind=kLoop, calls=%fused_computation.35.clone.1 | loop fusion | flops 37748736 | bytes 17302048 | tf_op jit(solution)/shard_map/convert
  443.9 5.9 fusion.84
  469.5 63.0 %fusion.83 = (bf16[8,1,32,64,128]{4,3,2,1,0:T(8,128)(2,1)S(1)}, bf16[8,1,32,64,128]{4,3,2,1,0:T(8,128)(2,1)S(1)}, bf16[8,1,32,64,128]{4,3,2,1,0:T(8,128)(2,1)S(1)}, bf16[8,1,32,64,128]{4,3,2,1,0:T(8,128)(2,1)S(1)}) fusion(f32[8,32,128]{2,1,0:T(8,128)S(1)} %gather_fusion.2, f32[8,32,128]{2,1,0:T(8,128)S(1)} %gather_fusion.3, ...), kind=kLoop, calls=%fused_computation.35.clone.1 | loop fusion | flops 37748736 | bytes 17302048 | tf_op jit(solution)/shard_map/convert
  536.5 5.9 fusion.84
  562.1 63.0 %fusion.83 = (bf16[8,1,32,64,128]{4,3,2,1,0:T(8,128)(2,1)S(1)}, bf16[8,1,32,64,128]{4,3,2,1,0:T(8,128)(2,1)S(1)}, bf16[8,1,32,64,128]{4,3,2,1,0:T(8,128)(2,1)S(1)}, bf16[8,1,32,64,128]{4,3,2,1,0:T(8,128)(2,1)S(1)}) fusion(f32[8,32,128]{2,1,0:T(8,128)S(1)} %gather_fusion.2, f32[8,32,128]{2,1,0:T(8,128)S(1)} %gather_fusion.3, ...), kind=kLoop, calls=%fused_computation.35.clone.1 | loop fusion | flops 37748736 | bytes 17302048 | tf_op jit(solution)/shard_map/convert
  629.1 5.9 fusion.84
  654.7 63.0 %fusion.83 = (bf16[8,1,32,64,128]{4,3,2,1,0:T(8,128)(2,1)S(1)}, bf16[8,1,32,64,128]{4,3,2,1,0:T(8,128)(2,1)S(1)}, bf16[8,1,32,64,128]{4,3,2,1,0:T(8,128)(2,1)S(1)}, bf16[8,1,32,64,128]{4,3,2,1,0:T(8,128)(2,1)S(1)}) fusion(f32[8,32,128]{2,1,0:T(8,128)S(1)} %gather_fusion.2, f32[8,32,128]{2,1,0:T(8,128)S(1)} %gather_fusion.3, ...), kind=kLoop, calls=%fused_computation.35.clone.1 | loop fusion | flops 37748736 | bytes 17302048 | tf_op jit(solution)/shard_map/convert
  721.7 5.9 fusion.84
  747.2 63.0 %fusion.83 = (bf16[8,1,32,64,128]{4,3,2,1,0:T(8,128)(2,1)S(1)}, bf16[8,1,32,64,128]{4,3,2,1,0:T(8,128)(2,1)S(1)}, bf16[8,1,32,64,128]{4,3,2,1,0:T(8,128)(2,1)S(1)}, bf16[8,1,32,64,128]{4,3,2,1,0:T(8,128)(2,1)S(1)}) fusion(f32[8,32,128]{2,1,0:T(8,128)S(1)} %gather_fusion.2, f32[8,32,128]{2,1,0:T(8,128)S(1)} %gather_fusion.3, ...), kind=kLoop, calls=%fused_computation.35.clone.1 | loop fusion | flops 37748736 | bytes 17302048 | tf_op jit(solution)/shard_map/convert
  814.3 5.9 fusion.84
  839.8 63.0 %fusion.83 = (bf16[8,1,32,64,128]{4,3,2,1,0:T(8,128)(2,1)S(1)}, bf16[8,1,32,64,128]{4,3,2,1,0:T(8,128)(2,1)S(1)}, bf16[8,1,32,64,128]{4,3,2,1,0:T(8,128)(2,1)S(1)}, bf16[8,1,32,64,128]{4,3,2,1,0:T(8,128)(2,1)S(1)}) fusion(f32[8,32,128]{2,1,0:T(8,128)S(1)} %gather_fusion.2, f32[8,32,128]{2,1,0:T(8,128)S(1)} %gather_fusion.3, ...), kind=kLoop, calls=%fused_computation.35.clone.1 | loop fusion | flops 37748736 | bytes 17302048 | tf_op jit(solution)/shard_map/convert
  906.9 5.9 fusion.84
  932.4 63.0 %fusion.83 = (bf16[8,1,32,64,128]{4,3,2,1,0:T(8,128)(2,1)S(1)}, bf16[8,1,32,64,128]{4,3,2,1,0:T(8,128)(2,1)S(1)}, bf16[8,1,32,64,128]{4,3,2,1,0:T(8,128)(2,1)S(1)}, bf16[8,1,32,64,128]{4,3,2,1,0:T(8,128)(2,1)S(1)}) fusion(f32[8,32,128]{2,1,0:T(8,128)S(1)} %gather_fusion.2, f32[8,32,128]{2,1,0:T(8,128)S(1)} %gather_fusion.3, ...), kind=kLoop, calls=%fused_computation.35.clone.1 | loop fusion | flops 37748736 | bytes 17302048 | tf_op jit(solution)/shard_map/convert
  999.4 5.9 fusion.84
  1025.0 63.0 %fusion.83 = (bf16[8,1,32,64,128]{4,3,2,1,0:T(8,128)(2,1)S(1)}, bf16[8,1,32,64,128]{4,3,2,1,0:T(8,128)(2,1)S(1)}, bf16[8,1,32,64,128]{4,3,2,1,0:T(8,128)(2,1)S(1)}, bf16[8,1,32,64,128]{4,3,2,1,0:T(8,128)(2,1)S(1)}) fusion(f32[8,32,128]{2,1,0:T(8,128)S(1)} %gather_fusion.2, f32[8,32,128]{2,1,0:T(8,128)S(1)} %gather_fusion.3, ...), kind=kLoop, calls=%fused_computation.35.clone.1 | loop fusion | flops 37748736 | bytes 17302048 | tf_op jit(solution)/shard_map/convert
  1092.0 5.9 fusion.84
  1117.6 63.0 %fusion.83 = (bf16[8,1,32,64,128]{4,3,2,1,0:T(8,128)(2,1)S(1)}, bf16[8,1,32,64,128]{4,3,2,1,0:T(8,128)(2,1)S(1)}, bf16[8,1,32,64,128]{4,3,2,1,0:T(8,128)(2,1)S(1)}, bf16[8,1,32,64,128]{4,3,2,1,0:T(8,128)(2,1)S(1)}) fusion(f32[8,32,128]{2,1,0:T(8,128)S(1)} %gather_fusion.2, f32[8,32,128]{2,1,0:T(8,128)S(1)} %gather_fusion.3, ...), kind=kLoop, calls=%fused_computation.35.clone.1 | loop fusion | flops 37748736 | bytes 17302048 | tf_op jit(solution)/shard_map/convert
  1184.6 5.9 fusion.84
  1193.2 14.8 bitcast_multiply_fusion
  1208.0 673.3 %reduce-scatter.2.cloned.1.call-done = f32[4,128,128]{2,1,0:T(8,128)} async-done(((f32[512,128,128]{2,1,0:T(8,128)}), f32[4,128,128]{2,1,0:T(8,128)}) %reduce-scatter.2.cloned.1.call-update) | async-done | bytes 262160 | tf_op jit(solution)/shard_map/reduce_scatter | solution.py:139
  (326 shorter events, 302.9 us)
Async XLA Ops:
  6.5 10.3 copy-start
  6.5 47.1 %all-gather.3.cloned.1.call-start = ((), (), s32[]{:S(2)}) async-start(), calls=%async_computation.2 | async-start | bytes 1114112 | tf_op jit(solution)/shard_map/all_gather | solution.py:72
  7.3 1874.0 %reduce-scatter.2.cloned.1.call-start = ((), (), s32[]{:S(2)}) async-start(), calls=%async_computation.1 | async-start | bytes 33816576 | tf_op jit(solution)/shard_map/reduce_scatter | solution.py:139
  1208.0 673.3 %copy-start.1 = (s32[1,16,16,16]{3,2,1,0:T(8,128)S(1)}, s32[1,16,16,16]{3,2,1,0:T(8,128)}, u32[]{:S(2)}) copy-start(s32[1,16,16,16]{3,2,1,0:T(8,128)} %param.13) | copy-start | bytes 49156
Sparse Core Ops, SparseCore 0:
  9.5 44.0 all-gather.2
  1208.1 673.1 reduce-scatter.1
where the time goes:
time: 1920 us; the launch traced here: 1890 us
  other arithmetic  916 us (48%)
  waiting for transfers between devices  705 us (37%)
  local copies, waits for them, and re-layouts  161 us (8%)
  matrix products  85 us (4%)
    another operation x12, other arithmetic  755 us
    reduce_scatter x1, waiting for transfers between devices, body(): lax.psum_scatter((buffer[:, None] * placed[:, :, None, None]).reshape(til...  673 us
    dot_general x12, matrix products, one_block(): jnp.einsum('brz,brx->bzx', depth_factor, lateral_factor, preferred_elemen...  70.3 us
    convert_element_type x12, other arithmetic, body(): alive_flag = (slot_local < foot_count[0][centre_local]).astype(jnp.int32)  58.6 us
    another operation x12, other arithmetic, pair_factors(): jnp.stack([part_real, -part_imag], axis=1).astype(jnp.bfloat16)  48.8 us
  transfers between devices with their start and end apart: 2, of which 2 were waited for; matrix products, arithmetic and copies ran while one was open for 1% of the time, Pallas kernels for 0%

commit v1 on v0

v1 whole, which is shorter than its diff:
```python
import math, functools
import numpy as np
import jax, jax.numpy as jnp
from jax import lax
from jax.experimental import pallas as pl
from jax.experimental.pallas import tpu as pltpu

TWO_PI = 2*math.pi

def fit():
    import numpy.polynomial.chebyshev as ch, numpy.polynomial.polynomial as po
    x = np.cos(np.pi*(np.arange(400)+.5)/400)
    q = (x*0.5+0.5)*0.25
    a = 2*np.pi*np.sqrt(q)
    def f(y, deg):
        c = ch.Chebyshev.fit(q, y, deg, domain=[0, 0.25])
        return [float(v) for v in c.convert(kind=po.Polynomial).coef]
    return f(np.cos(a), 7), f(np.sin(a)/np.sqrt(q), 6)
CC, SC = fit()

def sincos_turns(t):
    r = t - jnp.round(t)
    q = r * r
    cs = CC[-1]
    for c in CC[-2::-1]:
        cs = cs * q + c
    sn = SC[-1]
    for c in SC[-2::-1]:
        sn = sn * q + c
    return cs, sn * r

NE, NS, NF, NP, NC = 10, 8, 64, 32, 8
W0 = 4.0; DW = 60.0/64; MID = 32

def lateral(tl_ref, sp_ref, l_scr, e):
    tl = tl_ref[e]; sp = sp_ref[e]
    lc, ls = sincos_turns(W0*tl)
    dm = jnp.exp(sp*(-TWO_PI*W0))
    lr = lc*dm; li = -(ls*dm)
    uc, us = sincos_turns(DW*tl)
    du = jnp.exp(sp*(-TWO_PI*DW))
    ur = uc*du; ui = -(us*du)
    for f in range(NF):
        l_scr[e, 0, f] = lr.astype(jnp.bfloat16)
        l_scr[e, 1, f] = li.astype(jnp.bfloat16)
        if f < NF-1:
            lr, li = lr*ur - li*ui, lr*ui + li*ur

def depth_unit(c, d_scr, i, tdt, bt):
    z = pl.ds(pl.multiple_of(i*16, 16), 16)
    seeds = []
    for h in range(2):
        td = tdt[h, z, :]
        c1, s1 = sincos_turns((W0+DW*MID)*td)
        uc, us = sincos_turns(DW*td)
        seeds.append((c1*uc + s1*us, s1*uc - c1*us, c1, s1, uc+uc))
    def emit(f, st):
        ar = ai = None
        for h in range(2):
            br = bt[c, h, pl.ds(f, 1), :]
            bi = bt[c, h, pl.ds(NF+f, 1), :]
            C, S = st[h][2], st[h][3]
            xr = br*C - bi*S
            xi = br*S + bi*C
            ar = xr if ar is None else ar + xr
            ai = xi if ai is None else ai + xi
        d_scr[0, z, f*128:f*128+128] = ar.astype(jnp.bfloat16)
        d_scr[1, z, f*128:f*128+128] = ai.astype(jnp.bfloat16)
    def step(st):
        return [(x[2], x[3], sd[4]*x[2]-x[0], sd[4]*x[3]-x[1]) for x, sd in zip(st, seeds)]
    st = [sd[:4] for sd in seeds]
    for f in range(MID, NF):
        emit(f, st)
        if f < NF-1: st = step(st)
    st = [(sd[2], sd[3], sd[0], sd[1]) for sd in seeds]
    for f in range(MID-1, -1, -1):
        emit(f, st)
        if f > 0: st = step(st)

def mm_unit(e, d_scr, i, l_scr, acc):
    k = pl.ds(pl.multiple_of(i*1024, 1024), 1024)
    o = acc[...]
    for part in range(2):
        l8 = l_scr[e, part, pl.ds(i*8, 8)]
        rhs = jnp.concatenate([l8[j] for j in range(8) for _ in range(4)], 0)
        o = o + jnp.dot(d_scr[part, :, k], rhs, preferred_element_type=jnp.float32)
    acc[...] = o

def main_kernel(cen_ref, td_ref, tl_ref, sp_ref, b_ref, out_ref, tdt, bt, d0, d1, l_scr, acc):
    def bprep(c, _):
        for h in range(2):
            bt[c, h] = b_ref[c, h].T
        return 0
    lax.fori_loop(0, NC, bprep, 0)
    def lprep(e, _):
        lateral(tl_ref, sp_ref, l_scr, e)
        return 0
    lax.fori_loop(0, NE, lprep, 0)
    def prep(e):
        for h in range(2):
            tdt[h] = td_ref[e, h].T
    def both(e, dst, src):
        c = cen_ref[e]
        prep(e)
        acc[...] = jnp.zeros_like(acc)
        def u(i, _):
            if src is not None:
                mm_unit(e-1, src, i, l_scr, acc)
            depth_unit(c, dst, i, tdt, bt)
            return 0
        lax.fori_loop(0, 8, u, 0)
        if src is not None:
            out_ref[e-1] = acc[...]
    both(0, d0, None)
    def pair(k, _):
        both(2*k+1, d1, d0)
        both(2*k+2, d0, d1)
        return 0
    lax.fori_loop(0, NE//2-1, pair, 0)
    both(NE-1, d1, d0)
    acc[...] = jnp.zeros_like(acc)
    def ul(i, _):
        mm_unit(NE-1, d1, i, l_scr, acc)
        return 0
    lax.fori_loop(0, 8, ul, 0)
    out_ref[NE-1] = acc[...]

def main_call(cen, td, tl, sp, b):
    vm = pl.BlockSpec(memory_space=pltpu.VMEM)
    return pl.pallas_call(
        main_kernel,
        out_shape=jax.ShapeDtypeStruct((NE, 128, 128), jnp.float32),
        in_specs=[pl.BlockSpec(memory_space=pltpu.SMEM), vm, vm, vm, vm],
        out_specs=vm,
        scratch_shapes=[pltpu.VMEM((2, 128, 128), jnp.float32), pltpu.VMEM((NC, 2, 128, 128), jnp.float32),
                        pltpu.VMEM((2, 128, NF*128), jnp.bfloat16), pltpu.VMEM((2, 128, NF*128), jnp.bfloat16), pltpu.VMEM((NE, 2, NF, 32, 128), jnp.bfloat16),
                        pltpu.VMEM((128, 128), jnp.float32)],
        name="maincore",
        compiler_params=pltpu.CompilerParams(vmem_limit_bytes=60*1024*1024),
    )(cen, td, tl, sp, b)


from jax.sharding import PartitionSpec as P

FOOT = 12
LIVE = 80


def slant_tables():
    freq_index = jnp.arange(NF, dtype=jnp.float32)
    angular = 2.0 * math.pi * (4.0 + 60.0 * freq_index / NF)
    centred = jnp.arange(32, dtype=jnp.float32) - 0.5 * 31
    taper = jnp.exp(-((centred / 8.0) ** 2)) / math.sqrt(32)
    slowness = 2e-05 * (jnp.arange(NP, dtype=jnp.float32) - 0.5 * 31)
    angle = angular[:, None, None] * slowness[None, :, None] * (25.0 * centred)[None, None, :]
    return (taper * jnp.cos(angle)).astype(jnp.bfloat16), (-taper * jnp.sin(angle)).astype(jnp.bfloat16)


def pick(index, table):
    n = table.shape[0]
    hit = index[:, None] == jnp.arange(n, dtype=jnp.int32)[None, :]
    return jnp.sum(jnp.where(hit, table[None, :], 0), axis=1)


def body(traces, send_table, window_slots, ray_depth, ray_lateral, ray_spread, ray_index, foot_count, foot_tiles, tile_owner):
    group = lax.axis_index("beam")
    shot = lax.axis_index("shot")
    incl = jnp.cumsum(foot_count[0])
    n = jnp.arange(LIVE, dtype=jnp.int32)
    cen = jnp.sum((incl[None, :] <= n[:, None]).astype(jnp.int32), axis=1)
    first = pick(cen, incl - foot_count[0])
    eid = cen * FOOT + (n - first)
    rows = pick(eid, ray_index.reshape(-1))
    tiles = pick(eid, lax.dynamic_slice_in_dim(foot_tiles, group * NC, NC, 0).reshape(-1))
    owner = pick(tiles, tile_owner)
    stack_real, stack_imag = slant_tables()
    all_rows = lax.all_gather(traces[0], "beam", axis=0, tiled=True)
    my_routes = lax.dynamic_index_in_dim(send_table[0], group, 1, keepdims=False)
    flat = (jnp.arange(16, dtype=jnp.int32)[:, None] * 256 + my_routes).reshape(-1)
    arrived = all_rows[flat]
    win = arrived[window_slots[0].reshape(-1)].reshape(NC, 32, 128)
    tr, ti = win[..., :NF], win[..., NF:]
    def es(a, b):
        return jnp.einsum("fpk,ckf->cpf", a, b, preferred_element_type=jnp.float32)
    br = es(stack_real, tr) - es(stack_imag, ti)
    bi = es(stack_real, ti) + es(stack_imag, tr)
    beam = jnp.concatenate([br, bi], axis=2) * (1.0 / math.sqrt(2048.0))
    beam_all = lax.all_gather(beam, "shot", axis=1)
    beam_all = beam_all.reshape(NC, 2, 128, 128)
    td = lax.all_to_all(ray_depth[0][rows].reshape(8, NE, 32, 128), "shot", 0, 1, tiled=False)
    td = td.reshape(NE, 2, 128, 128)
    mine = lax.dynamic_slice_in_dim(rows, shot * NE, NE, 0)
    tl = ray_lateral[mine]
    sp = ray_spread[mine]
    part = main_call(lax.dynamic_slice_in_dim(cen, shot * NE, NE, 0), td, tl, sp, beam_all)
    part = lax.all_gather(part.astype(jnp.bfloat16), "shot", axis=0, tiled=True)
    want = shot * 16 + jnp.arange(16, dtype=jnp.int32)
    sel = (owner[None, :] == want[:, None]).astype(jnp.bfloat16)
    dense = jnp.dot(sel, part.reshape(LIVE, 128 * 128), preferred_element_type=jnp.float32).astype(jnp.bfloat16)
    dense = dense.reshape(16, 128, 128)
    got = lax.all_to_all(dense, "beam", 0, 0, tiled=False).reshape(16, 128 * 128)
    me = shot * 16 + group
    same = tile_owner == me
    t = jnp.arange(512, dtype=jnp.int32)
    rank = jnp.cumsum(same.astype(jnp.int32)) - 1
    slot_of = jnp.where(same, rank, -1)
    ft = foot_tiles.reshape(16, NC * FOOT)
    slot = jnp.max(pick(ft.reshape(-1), slot_of).reshape(16, NC * FOOT), axis=1)
    place = (slot[None, :] == jnp.arange(4, dtype=jnp.int32)[:, None]).astype(jnp.bfloat16)
    out = jnp.dot(place, got, preferred_element_type=jnp.float32)
    return out.reshape(4, 128, 128)


def solution(mesh):
    in_specs = (
        P("shot", "beam", None),
        P("shot", None, None, None),
        P("shot", "beam", None),
        P("shot", "beam", None, None),
        P("beam", None, None),
        P("beam", None, None),
        P("beam", None),
        P("beam", None),
        P(),
        P(),
    )
    return jax.shard_map(body, mesh=mesh, in_specs=in_specs, out_specs=P(("shot", "beam"), None, None), check_vma=False)
```

time: 1920 us -> 231 us (0.12); the launches traced: 1890 us -> 230 us
  other arithmetic: 916 us -> 6.11 us
  waiting for transfers between devices: 705 us -> 91.8 us
  local copies, waits for them, and re-layouts: 161 us -> 22.1 us
  matrix products: 85 us -> 18.3 us
  Pallas kernels: 0 us -> 65.4 us
    another operation x24 -> x4, other arithmetic: 804 us -> 1.18 us
    reduce_scatter x1 -> x0, waiting for transfers between devices: 673 us -> none  [body(): lax.psum_scatter((buffer[:, None] * placed[:, :, None, None]).reshape(til...]
    gather x113 -> x5, local copies, waits for them, and re-layouts: 151 us -> 13.7 us  [the longest x1 3.88 us: body(): ray_depth[0][rows].reshape(8, NE, 32, 128)]
    dot_general x16 -> x6, matrix products: 85 us -> 18.3 us  [the longest x4 14.7 us: es(): return jnp.einsum('fpk,ckf->cpf', a, b, preferred_element_type=jnp.float32)]
    pallas_call x0 -> x1, Pallas kernels: none -> 65.4 us  [main_call(): pl.pallas_call(main_kernel, out_shape=jax.ShapeDtypeStruct((NE, 128, 128)...]
    convert_element_type x13 -> x1, other arithmetic: 58.7 us -> 1.86 us  [body(): part = lax.all_gather(part.astype(jnp.bfloat16), 'shot', axis=0, tiled=True)]
    all_gather x1 -> x3, waiting for transfers between devices: 31.1 us -> 66.9 us  [the longest x1 43.4 us: body(): all_rows = lax.all_gather(traces[0], 'beam', axis=0, tiled=True)]
    scatter-add x12 -> x0, other arithmetic: 32.5 us -> none  [one_block(): return (buffer.at[entry_owner[chosen]].add(contribution), None)]
  transfers between devices with their start and end apart: 2 -> 5, of which waited for: 2 -> 4; matrix products, arithmetic and copies ran while one was open for 1% -> 8% of each run, Pallas kernels for 0% -> 0%
where the time goes in v1:
time: 231 us; the launch traced here: 230 us
  waiting for transfers between devices  91.8 us (40%)
  Pallas kernels  65.4 us (28%)
  local copies, waits for them, and re-layouts  22.1 us (10%)
  matrix products  18.3 us (8%)
  starting transfers between devices  13.5 us (6%)
  between operations  13.3 us (6%)
  other arithmetic  6.11 us (3%)
    pallas_call x1, Pallas kernels, main_call(): pl.pallas_call(main_kernel, out_shape=jax.ShapeDtypeStruct((NE, 128, 128)...  65.4 us
    all_gather x1, waiting for transfers between devices, body(): all_rows = lax.all_gather(traces[0], 'beam', axis=0, tiled=True)  43.4 us
    all_gather x1, waiting for transfers between devices, body(): part = lax.all_gather(part.astype(jnp.bfloat16), 'shot', axis=0, tiled=True)  23.5 us
    dot_general x4, matrix products, es(): return jnp.einsum('fpk,ckf->cpf', a, b, preferred_element_type=jnp.float32)  14.7 us
    all_to_all x1, waiting for transfers between devices, body(): lax.all_to_all(ray_depth[0][rows].reshape(8, NE, 32, 128), 'shot', 0, 1,...  14.4 us
    all_to_all x1, waiting for transfers between devices, body(): lax.all_to_all(dense, 'beam', 0, 0, tiled=False).reshape(16, 128 * 128)  9.79 us
    all_to_all x1, starting transfers between devices, body(): lax.all_to_all(ray_depth[0][rows].reshape(8, NE, 32, 128), 'shot', 0, 1,...  6.71 us
    all_to_all x1, starting transfers between devices, body(): lax.all_to_all(dense, 'beam', 0, 0, tiled=False).reshape(16, 128 * 128)  6.7 us
  transfers between devices with their start and end apart: 5, of which 4 were waited for; matrix products, arithmetic and copies ran while one was open for 8% of the time, Pallas kernels for 0%

profile of v1, /device:TPU:1, one launch (start us, length us, event | category | flops | bytes accessed | tf_op | source)
XLA Modules:
  0.0 230.4 jit_solution(11658643556632534482)
XLA Ops:
  6.5 0.7 all-gather.9.cloned.1.call-update
  7.3 0.8 reduce-window.18
  8.4 0.8 reshape_squeeze.7
  9.4 0.7 fusion.40
  10.2 43.4 %all-gather.9.cloned.1.call-done = bf16[1,4096,128]{2,1,0:T(8,128)(2,1)} async-done(((bf16[1,256,128]{2,1,0:T(8,128)(2,1)}), bf16[1,4096,128]{2,1,0:T(8,128)(2,1)}) %all-gather.9.cloned.1.call-update) | async-done | bytes 1048592 | tf_op jit(solution)/shard_map/all_gather | solution.py:177
  53.6 2.1 gather_fusion.3
  55.7 0.9 gather_fusion.4
  56.9 3.6 %fusion.13 = f32[64,8,32]{2,1,0:T(8,128)S(1)} fusion(bf16[8,32,64]{1,0,2:T(8,128)(2,1)S(1)} %copy.58, f32[32]{0:T(128)S(1)} %get-tuple-element.12, f32[64,32]{1,0:T(8,128)S(1)} %broadcast_multiply_fusion, f32[32]{0:T(128)S(1)} %get-tuple-element.11), kind=kOutput, calls=%fused_computation.19 | convolution fusion | flops 1245184 | bytes 106752 | tf_op jit(solution)/shard_map/fpk,ckf->cpf/dot_general | solution.py:184
  60.5 3.6 %fusion.15 = f32[64,8,32]{2,1,0:T(8,128)S(1)} fusion(bf16[8,32,64]{1,0,2:T(8,128)(2,1)S(1)} %copy.57, f32[32]{0:T(128)S(1)} %get-tuple-element.12, f32[64,32]{1,0:T(8,128)S(1)} %broadcast_multiply_fusion, f32[32]{0:T(128)S(1)} %get-tuple-element.11), kind=kOutput, calls=%fused_computation.20 | convolution fusion | flops 1245184 | bytes 106752 | tf_op jit(solution)/shard_map/fpk,ckf->cpf/dot_general | solution.py:184
  64.1 3.8 %fusion.9 = f32[64,8,32]{2,1,0:T(8,128)S(1)} fusion(bf16[8,32,64]{1,0,2:T(8,128)(2,1)S(1)} %copy.57, f32[32]{0:T(128)S(1)} %fusion.43, f32[32]{0:T(128)S(1)} %get-tuple-element.12, f32[64,32]{1,0:T(8,128)S(1)} %broadcast_multiply_fusion), kind=kOutput, calls=%fused_computation.17 | convolution fusion | flops 1245184 | bytes 106752 | tf_op jit(solution)/shard_map/fpk,ckf->cpf/dot_general | solution.py:184
  67.9 3.6 %fusion.11 = f32[64,8,32]{2,1,0:T(8,128)S(1)} fusion(bf16[8,32,64]{1,0,2:T(8,128)(2,1)S(1)} %copy.58, f32[32]{0:T(128)S(1)} %fusion.43, f32[32]{0:T(128)S(1)} %get-tuple-element.12, f32[64,32]{1,0:T(8,128)S(1)} %broadcast_multiply_fusion), kind=kOutput, calls=%fused_computation.18 | convolution fusion | flops 1245184 | bytes 106752 | tf_op jit(solution)/shard_map/fpk,ckf->cpf/dot_general | solution.py:184
  72.2 0.8 fusion.32
  73.3 0.2 select_reduce_fusion.3
  73.5 3.9 %gather_fusion = f32[80,32,128]{2,1,0:T(8,128)} fusion(f32[256,32,128]{2,1,0:T(8,128)} %bitcast.72, s32[1024]{0:T(1024)S(1)} %pad_clamp_fusion.3), kind=kCustom, calls=%fused_computation | custom fusion | bytes 2621760 | tf_op jit(solution)/shard_map/gather | solution.py:190
  77.4 6.7 %all-to-all-start = ((f32[8,10,1,32,128]{4,3,1,2,0:T(8,128)}), f32[8,10,1,32,128]{4,3,1,2,0:T(8,128)S(1)}, u32[]{:S(2)}, u32[]{:S(2)}) async-start(f32[8,10,1,32,128]{4,3,1,2,0:T(8,128)} %bitcast.10), calls=%async_computation | async-start | bytes 2621440 | tf_op jit(solution)/shard_map/all_to_all | solution.py:190
  84.1 0.5 dynamic_slice.14.cen_ref
  84.8 3.4 %gather_fusion.1 = f32[10,32,128]{2,1,0:T(8,128)} fusion(f32[256,32,128]{2,1,0:T(8,128)} %param.14, s32[1024]{0:T(1024)S(1)} %pad_clamp_fusion.2), kind=kCustom, calls=%fused_computation.1 | custom fusion | bytes 327720 | tf_op jit(solution)/shard_map/gather | solution.py:193
  88.2 3.4 %gather_fusion.2 = f32[10,32,128]{2,1,0:T(8,128)} fusion(f32[256,32,128]{2,1,0:T(8,128)} %param.15, s32[1024]{0:T(1024)S(1)} %pad_clamp_fusion.2), kind=kCustom, calls=%fused_computation.2 | custom fusion | bytes 327720 | tf_op jit(solution)/shard_map/gather | solution.py:194
  91.6 14.4 %all-to-all-done = f32[8,10,1,32,128]{4,3,1,2,0:T(8,128)S(1)} async-done(((f32[8,10,1,32,128]{4,3,1,2,0:T(8,128)}), f32[8,10,1,32,128]{4,3,1,2,0:T(8,128)S(1)}, u32[]{:S(2)}, u32[]{:S(2)}) %all-to-all-start) | async-done | bytes 1310752 | tf_op jit(solution)/shard_map/all_to_all | solution.py:190
  106.0 1.2 copy.46
  107.2 2.3 copy.54
  109.4 65.4 %maincore.1 = f32[10,128,128]{2,1,0:T(8,128)} custom-call(s32[10]{0:T(128)} %dynamic_slice.14.cen_ref, f32[10,2,128,128]{3,2,1,0:T(8,128)} %bitcast.67, f32[10,32,128]{2,1,0:T(8,128)} %gather_fusion.1, f32[10,32,128]{2,1,0:T(8,128)} %gather_fusion.2, f32[8,2,128,128]{3,2,1,0:T(8,128)} %bitcast.68), custom_call_target="tpu_custom_call" | custom-call | tf_op jit(solution)/shard_map/maincore/pallas_call | solution.py:130
  174.9 1.9 convert_element_type.25
  176.9 0.3 reduce-window.11
  177.6 23.5 %all-gather.7.cloned.1.call-done = bf16[80,128,128]{2,1,0:T(8,128)(2,1)} async-done(((bf16[10,128,128]{2,1,0:T(8,128)(2,1)}), bf16[80,128,128]{2,1,0:T(8,128)(2,1)}) %all-gather.7.cloned.1.call-update) | async-done | bytes 2621456 | tf_op jit(solution)/shard_map/all_gather | solution.py:196
  201.1 3.2 %fusion.2 = bf16[2,8,128,128]{3,1,2,0:T(8,128)(2,1)S(1)} fusion(bf16[10,8,128,128]{3,2,1,0:T(8,128)(2,1)} %bitcast.69, s32[80]{0:T(128)S(1)} %select_reduce_fusion.1, s32[16]{0:T(128)S(1)} %iota_add_fusion.1), kind=kOutput, calls=%fused_computation.12 | convolution fusion | flops 42206464 | bytes 3146112 | tf_op jit(solution)/shard_map/dot_general | solution.py:199
  204.4 0.9 copy.61
  205.2 6.7 %all-to-all-start.1 = ((bf16[16,128,128]{2,1,0:T(8,128)(2,1)}), bf16[16,128,128]{2,1,0:T(8,128)(2,1)S(1)}, u32[]{:S(2)}, u32[]{:S(2)}) async-start(bf16[16,128,128]{2,1,0:T(8,128)(2,1)} %bitcast.33), calls=%async_computation.1 | async-start | bytes 1048576 | tf_op jit(solution)/shard_map/all_to_all | solution.py:201
  212.1 0.6 select_reduce_fusion
  213.0 9.8 %all-to-all-done.1 = bf16[16,128,128]{2,1,0:T(8,128)(2,1)S(1)} async-done(((bf16[16,128,128]{2,1,0:T(8,128)(2,1)}), bf16[16,128,128]{2,1,0:T(8,128)(2,1)S(1)}, u32[]{:S(2)}, u32[]{:S(2)}) %all-to-all-start.1) | async-done | bytes 524320 | tf_op jit(solution)/shard_map/all_to_all | solution.py:201
  222.8 0.4 fusion.17
  223.2 0.7 copy.56
  (59 shorter events, 3.0 us)
Async XLA Ops:
  6.5 1.8 copy-start
  6.5 47.0 %all-gather.9.cloned.1.call-start = ((), (), s32[]{:S(2)}) async-start(), calls=%async_computation.4 | async-start | bytes 1114112 | tf_op jit(solution)/shard_map/all_gather | solution.py:177
  7.3 99.9 %all-gather.5.cloned.1.call-start = ((), (), s32[]{:S(2)}) async-start(), calls=%async_computation.2 | async-start | bytes 1179648 | tf_op jit(solution)/shard_map/all_gather | solution.py:188
  60.5 12.5 %copy-start.1 = (s32[128,12]{0,1:T(8,128)S(1)}, s32[128,12]{0,1:T(8,128)}, u32[]{:S(2)}) copy-start(s32[128,12]{0,1:T(8,128)} %param.18) | copy-start | bytes 18436
  60.5 12.8 %copy-start.3 = (s32[8,12]{1,0:T(8,128)S(1)}, s32[8,12]{1,0:T(8,128)}, u32[]{:S(2)}) copy-start(s32[8,12]{1,0:T(8,128)} %param.16) | copy-start | bytes 1156
  77.4 28.6 %all-to-all-start = ((f32[8,10,1,32,128]{4,3,1,2,0:T(8,128)}), f32[8,10,1,32,128]{4,3,1,2,0:T(8,128)S(1)}, u32[]{:S(2)}, u32[]{:S(2)}) async-start(f32[8,10,1,32,128]{4,3,1,2,0:T(8,128)} %bitcast.10), calls=%async_computation | async-start | bytes 2621440 | tf_op jit(solution)/shard_map/all_to_all | solution.py:190
  84.1 117.0 %all-gather.7.cloned.1.call-start = ((), (), s32[]{:S(2)}) async-start(), calls=%async_computation.3 | async-start | bytes 2949120 | tf_op jit(solution)/shard_map/all_gather | solution.py:196
  107.1 69.7 %copy-start.2 = (s32[512]{0:T(512)S(1)}, s32[512]{0:T(512)}, u32[]{:S(2)}) copy-start(s32[512]{0:T(512)} %param.19) | copy-start | bytes 6148
  205.2 17.5 %all-to-all-start.1 = ((bf16[16,128,128]{2,1,0:T(8,128)(2,1)}), bf16[16,128,128]{2,1,0:T(8,128)(2,1)S(1)}, u32[]{:S(2)}, u32[]{:S(2)}) async-start(bf16[16,128,128]{2,1,0:T(8,128)(2,1)} %bitcast.33), calls=%async_computation.1 | async-start | bytes 1048576 | tf_op jit(solution)/shard_map/all_to_all | solution.py:201
Sparse Core Ops, SparseCore 0:
  9.5 44.0 all-gather.8
  73.1 27.0 all-gather.4
  176.9 24.1 all-gather.6

commit v2 on v1

v2 whole, which is shorter than its diff:
```python
import math

import jax
import jax.numpy as jnp
import numpy as np
from jax import lax
from jax.experimental import pallas as pl
from jax.experimental.pallas import tpu as pltpu
from jax.sharding import PartitionSpec as P

MESH = pl.DeviceIdType.MESH
F32, BF16 = jnp.float32, jnp.bfloat16
NF, NP, NC, WIN, FOOT, LIVE = 64, 32, 8, 32, 12, 80
NS, NG, NE = 8, 16, 10
W0, DW, MID = 4.0, 60.0 / 64, 32
TWO_PI = 2.0 * math.pi
KP = 16
AT_ROW, AT_CEN, AT_PICK, AT_SLOT = 0, LIVE, 2 * LIVE, 2 * LIVE + NG * NC


def fit():
    x = np.cos(np.pi * (np.arange(400) + 0.5) / 400)
    q = (x * 0.5 + 0.5) * 0.25
    a = 2 * np.pi * np.sqrt(q)

    def poly(y, deg):
        c = np.polynomial.chebyshev.Chebyshev.fit(q, y, deg, domain=[0, 0.25])
        return [float(v) for v in c.convert(kind=np.polynomial.Polynomial).coef]

    return poly(np.cos(a), 7), poly(np.sin(a) / np.sqrt(q), 6)


COS_C, SIN_C = fit()


def sincos_turns(t):
    r = t - jnp.round(t)
    q = r * r
    cs = COS_C[-1]
    for c in COS_C[-2::-1]:
        cs = cs * q + c
    sn = SIN_C[-1]
    for c in SIN_C[-2::-1]:
        sn = sn * q + c
    return cs, sn * r


def stack_tables():
    f32 = np.float32
    angular = (2.0 * math.pi * (4.0 + 60.0 * np.arange(NF, dtype=f32) / NF)).astype(f32)
    centred = np.arange(WIN, dtype=f32) - f32(0.5 * (WIN - 1))
    taper = (np.exp(-((centred / f32(8.0)) ** 2)) / f32(math.sqrt(WIN))).astype(f32)
    slow = (f32(2e-05) * (np.arange(NP, dtype=f32) - f32(15.5))).astype(f32)
    angle = (angular[None, None, :] * slow[None, :, None]) * (f32(25.0) * centred)[:, None, None]
    sr = (taper[:, None, None] * np.cos(angle)).astype(BF16)
    si = (-taper[:, None, None] * np.sin(angle)).astype(BF16)
    return np.concatenate([sr, sr], 2), np.concatenate([-si, si], 2)


def lateral(tl, sp, l_scr, e):
    lc, ls = sincos_turns(W0 * tl)
    dm = jnp.exp(sp * (-TWO_PI * W0))
    lr, li = lc * dm, -(ls * dm)
    uc, us = sincos_turns(DW * tl)
    du = jnp.exp(sp * (-TWO_PI * DW))
    ur, ui = uc * du, -(us * du)
    for f in range(NF):
        l_scr[e, 0, f] = lr.astype(BF16)
        l_scr[e, 1, f] = li.astype(BF16)
        if f < NF - 1:
            lr, li = lr * ur - li * ui, lr * ui + li * ur


def depth_unit(c, d_scr, i, tdt, bt):
    z = pl.ds(pl.multiple_of(i * 16, 16), 16)
    seeds = []
    for h in range(2):
        t = tdt[h, z, :]
        c1, s1 = sincos_turns((W0 + DW * MID) * t)
        uc, us = sincos_turns(DW * t)
        seeds.append((c1 * uc + s1 * us, s1 * uc - c1 * us, c1, s1, uc + uc))

    def emit(f, st):
        ar = ai = None
        for h in range(2):
            br = bt[c, h, f : f + 1, :]
            bi = bt[c, h, NF + f : NF + f + 1, :]
            cv, sv = st[h][2], st[h][3]
            xr = br * cv - bi * sv
            xi = br * sv + bi * cv
            ar = xr if ar is None else ar + xr
            ai = xi if ai is None else ai + xi
        d_scr[f, 0, z, :] = ar.astype(BF16)
        d_scr[f, 1, z, :] = ai.astype(BF16)

    def step(st):
        return [(x[2], x[3], s[4] * x[2] - x[0], s[4] * x[3] - x[1]) for x, s in zip(st, seeds)]

    st = [s[:4] for s in seeds]
    for f in range(MID, NF):
        emit(f, st)
        if f < NF - 1:
            st = step(st)
    st = [(s[2], s[3], s[0], s[1]) for s in seeds]
    for f in range(MID - 1, -1, -1):
        emit(f, st)
        if f > 0:
            st = step(st)


def mm_piece(e, d_scr, i, l_scr, acc):
    part = i % 2
    f0 = (i // 2) * KP
    l8 = l_scr[e, part, pl.ds(f0, KP)]
    rhs = jnp.concatenate([l8[j] for j in range(KP) for _ in range(4)], 0)
    lhs = jnp.concatenate([d_scr[f0 + j, part] for j in range(KP)], 1)
    acc[...] += jnp.dot(lhs, rhs, preferred_element_type=F32)


def kernel(
    tab, traces, send_col, win_col, t0, t1, depth_hbm, lat_hbm, spr_hbm, out_ref,
    depth_v, lat_v, spr_v, tr_out, tr_in, win_s, win_r, ball, bt, td_out, td_in, tdt,
    d0, d1, l_scr, acc, tiles, dense, got,
    tab_sem, loc_sem, trs, trr, bs, br_sem, tds, tdr, tls, tlr, ds_, dr,
):
    shot = lax.axis_index("shot")
    beam = lax.axis_index("beam")
    partner = shot + 1 - 2 * lax.rem(shot, 2)

    def at_shot(s):
        return dict(device_id={"shot": s, "beam": beam}, device_id_type=MESH)

    def at_beam(g):
        return dict(device_id={"shot": shot, "beam": g}, device_id_type=MESH)

    loads = [
        pltpu.make_async_copy(h, v, tab_sem.at[n])
        for n, (h, v) in enumerate(((depth_hbm, depth_v), (lat_hbm, lat_v), (spr_hbm, spr_v)))
    ]
    for cp in loads:
        cp.start()
    barrier = pltpu.get_barrier_semaphore()
    for d in range(1, NS):
        pl.semaphore_signal(barrier, inc=1, **at_shot(lax.rem(shot + d, NS)))
    for d in range(1, NG):
        pl.semaphore_signal(barrier, inc=1, **at_beam(lax.rem(beam + d, NG)))

    lanes = lax.broadcasted_iota(jnp.int32, (256, 256), 1)
    pick = jnp.where(lanes == send_col[...], 1.0, 0.0).astype(BF16)
    chosen = jnp.dot(pick, traces[...], preferred_element_type=F32).astype(BF16)
    tr_out[...] = chosen.reshape(NG, 16, 128)
    tr_in[beam] = tr_out[beam]

    loads[0].wait()

    def gather(e, _):
        for j in range(NS):
            td_out[j, e] = depth_v[tab[AT_ROW + j * NE + e]]
        return 0

    lax.fori_loop(0, NE, gather, 0)

    def own(e, _):
        td_in[e, shot] = td_out[shot, e]
        return 0

    lax.fori_loop(0, NE, own, 0)

    pl.semaphore_wait(barrier, NS - 1 + NG - 1)

    def trace_copy(d):
        g = lax.rem(beam + d, NG)
        return pltpu.make_async_remote_copy(
            src_ref=tr_out.at[g], dst_ref=tr_in.at[beam], send_sem=trs.at[d], recv_sem=trr.at[d], **at_beam(g)
        )

    def depth_copy(e, d):
        j = lax.rem(shot + d, NS)
        return pltpu.make_async_remote_copy(
            src_ref=td_out.at[j, e], dst_ref=td_in.at[e, shot], send_sem=tds.at[e, d], recv_sem=tdr.at[e, d], **at_shot(j)
        )

    for d in range(1, NG):
        trace_copy(d).start()
    for d in range(1, NS):
        depth_copy(0, d).start()

    loads[1].wait()
    loads[2].wait()

    def lat(e, _):
        r = tab[AT_ROW + shot * NE + e]
        lateral(lat_v[r], spr_v[r], l_scr, e)
        return 0

    lax.fori_loop(0, NE // 2, lat, 0)

    for d in range(1, NG):
        trace_copy(d).wait_recv()
    pick = jnp.where(lanes == win_col[...], 1.0, 0.0).astype(BF16)
    win = jnp.dot(pick, tr_in[...].reshape(256, 128), preferred_element_type=F32)
    win_s[...] = win.reshape(NC, WIN, 128)
    win_r[...] = pltpu.roll(win, 64, 1).reshape(NC, WIN, 128)

    def stack(c, _):
        a = jnp.zeros((NP, 128), F32)
        for k in range(WIN):
            a = a + (t0[k].astype(F32) * win_s[c, k : k + 1, :] + t1[k].astype(F32) * win_r[c, k : k + 1, :])
        ball[shot, c] = a * (1.0 / math.sqrt(NP * NF))
        return 0

    lax.fori_loop(0, NC, stack, 0)

    def beam_copy(slot, n, to):
        return pltpu.make_async_remote_copy(
            src_ref=ball.at[slot], dst_ref=ball.at[slot], send_sem=bs.at[n], recv_sem=br_sem.at[n], **at_shot(to)
        )

    sends = [beam_copy(shot, d, lax.rem(shot + 2 * d, NS)) for d in range(1, 4)]
    sends.append(beam_copy(shot, 0, partner))
    for cp in sends:
        cp.start()

    def rest(e, _):
        for d in range(1, NS):
            depth_copy(e, d).start()
        return 0

    lax.fori_loop(1, NE, rest, 0)
    lax.fori_loop(NE // 2, NE, lat, 0)
    for d in range(1, 4):
        sends[d - 1].wait_recv()
        cp = beam_copy(lax.rem(shot + NS - 2 * d, NS), 3 + d, partner)
        cp.start()
        sends.append(cp)
    for cp in sends[3:]:
        cp.wait_recv()

    def turn(c, _):
        for h in range(2):
            bt[c, h] = jnp.concatenate([ball[4 * h + s, c] for s in range(4)], 0).T
        return 0

    lax.fori_loop(0, NC, turn, 0)

    def tile_copy(e, d):
        n = shot * NE + e
        return pltpu.make_async_remote_copy(
            src_ref=tiles.at[n], dst_ref=tiles.at[n], send_sem=tls.at[e, d], recv_sem=tlr.at[e, d],
            **at_shot(lax.rem(shot + d, NS)),
        )

    def share(e):
        tiles[shot * NE + e] = acc[...].astype(BF16)
        for d in range(1, NS):
            tile_copy(e, d).start()

    def both(e, dst, src):
        c = tab[AT_CEN + shot * NE + e]
        for d in range(1, NS):
            depth_copy(e, d).wait_recv()
        for h in range(2):
            tdt[h] = td_in[e, 4 * h : 4 * h + 4].reshape(128, 128).T
        acc[...] = jnp.zeros_like(acc)

        def unit(i, _):
            if src is not None:
                mm_piece(e - 1, src, i, l_scr, acc)
            depth_unit(c, dst, i, tdt, bt)
            return 0

        lax.fori_loop(0, 8, unit, 0)
        if src is not None:
            share(e - 1)

    both(0, d0, None)

    def pair(k, _):
        both(2 * k + 1, d1, d0)
        both(2 * k + 2, d0, d1)
        return 0

    lax.fori_loop(0, NE // 2 - 1, pair, 0)
    both(NE - 1, d1, d0)
    acc[...] = jnp.zeros_like(acc)

    def last(i, _):
        mm_piece(NE - 1, d1, i, l_scr, acc)
        return 0

    lax.fori_loop(0, 8, last, 0)
    share(NE - 1)
    tiles[LIVE] = jnp.zeros((128, 128), BF16)

    def arrive(e, _):
        for d in range(1, NS):
            tile_copy(e, d).wait_recv()
        return 0

    lax.fori_loop(0, NE, arrive, 0)

    def gather_owner(b, _):
        s = tiles[tab[AT_PICK + b * NC]].astype(F32)
        for m in range(1, NC):
            s = s + tiles[tab[AT_PICK + b * NC + m]].astype(F32)
        dense[b] = s.astype(BF16)
        return 0

    lax.fori_loop(0, NG, gather_owner, 0)

    def owner_copy(d):
        g = lax.rem(beam + d, NG)
        return pltpu.make_async_remote_copy(
            src_ref=dense.at[g], dst_ref=got.at[beam], send_sem=ds_.at[d], recv_sem=dr.at[d], **at_beam(g)
        )

    for d in range(1, NG):
        owner_copy(d).start()
    got[beam] = dense[beam]
    for d in range(1, NG):
        owner_copy(d).wait_recv()
    for slot in range(4):
        out_ref[slot] = jnp.zeros((128, 128), F32)

    def place(g, _):
        v = got[g].astype(F32)
        at = tab[AT_SLOT + g]
        for slot in range(4):
            out_ref[slot] += v * jnp.where(at == slot, 1.0, 0.0)
        return 0

    lax.fori_loop(0, NG, place, 0)

    for d in range(1, NG):
        trace_copy(d).wait_send()
        owner_copy(d).wait_send()
    for cp in sends:
        cp.wait_send()

    def drain(e, _):
        for d in range(1, NS):
            depth_copy(e, d).wait_send()
            tile_copy(e, d).wait_send()
        return 0

    lax.fori_loop(0, NE, drain, 0)


def fused(tab, traces, send_col, win_col, depth, lat, spr):
    t0, t1 = stack_tables()
    vm = pl.BlockSpec(memory_space=pltpu.VMEM)
    hbm = pl.BlockSpec(memory_space=pl.ANY)
    dma = pltpu.SemaphoreType.DMA
    return pl.pallas_call(
        kernel,
        out_shape=jax.ShapeDtypeStruct((4, 128, 128), F32),
        in_specs=[pl.BlockSpec(memory_space=pltpu.SMEM), vm, vm, vm, vm, vm, hbm, hbm, hbm],
        out_specs=vm,
        scratch_shapes=[
            pltpu.VMEM((256, 32, 128), F32), pltpu.VMEM((256, 32, 128), F32), pltpu.VMEM((256, 32, 128), F32),
            pltpu.VMEM((NG, 16, 128), BF16), pltpu.VMEM((NG, 16, 128), BF16),
            pltpu.VMEM((NC, WIN, 128), F32), pltpu.VMEM((NC, WIN, 128), F32),
            pltpu.VMEM((NS, NC, NP, 128), F32), pltpu.VMEM((NC, 2, 128, 128), F32),
            pltpu.VMEM((NS, NE, NP, 128), F32), pltpu.VMEM((NE, NS, NP, 128), F32), pltpu.VMEM((2, 128, 128), F32),
            pltpu.VMEM((NF, 2, 128, 128), BF16), pltpu.VMEM((NF, 2, 128, 128), BF16),
            pltpu.VMEM((NE, 2, NF, NP, 128), BF16), pltpu.VMEM((128, 128), F32),
            pltpu.VMEM((LIVE + 1, 128, 128), BF16), pltpu.VMEM((NG, 128, 128), BF16), pltpu.VMEM((NG, 128, 128), BF16),
            dma((3,)), dma((1,)), dma((NG,)), dma((NG,)), dma((7,)), dma((7,)),
            dma((NE, NS)), dma((NE, NS)), dma((NE, NS)), dma((NE, NS)), dma((NG,)), dma((NG,)),
        ],
        compiler_params=pltpu.CompilerParams(
            collective_id=0, has_side_effects=True, vmem_limit_bytes=62 * 1024 * 1024
        ),
        name="beam_migration",
    )(tab, traces, send_col, win_col, jnp.asarray(t0), jnp.asarray(t1), depth, lat, spr)


def pick_from(index, table):
    hit = index[:, None] == jnp.arange(table.shape[0], dtype=jnp.int32)[None, :]
    return jnp.sum(jnp.where(hit, table[None, :], 0), axis=1)


def scalar_table(group, shot, ray_index, foot_count, foot_tiles, tile_owner):
    i32 = jnp.int32
    counts = foot_count[0]
    lower = jnp.arange(NC)[None, :] < jnp.arange(NC)[:, None]
    before = jnp.sum(jnp.where(lower, counts[None, :], 0), axis=1)
    n = jnp.arange(LIVE, dtype=i32)
    cen = jnp.sum(((before + counts)[None, :] <= n[:, None]).astype(i32), axis=1)
    eid = cen * FOOT + n - pick_from(cen, before)
    rows = pick_from(eid, ray_index.reshape(-1))
    mine = lax.dynamic_slice_in_dim(foot_tiles, group * NC, NC, 0).reshape(-1)
    owner = pick_from(pick_from(eid, mine), tile_owner)
    same = (owner[:, None] == owner[None, :]) & (n[None, :] < n[:, None])
    rank = jnp.sum(same.astype(i32), axis=1)
    key = (owner - shot * NG) * NC + rank
    hit = key[None, :] == jnp.arange(NG * NC, dtype=i32)[:, None]
    picks = LIVE + jnp.sum(jnp.where(hit, n[None, :] - LIVE, 0), axis=1)
    me = shot * NG + group
    t = jnp.arange(512, dtype=i32)
    held = tile_owner == me
    earlier = jnp.sum((held[None, :] & (t[None, :] < t[:, None])).astype(i32), axis=1)
    slot_of = jnp.where(held, earlier, 0)
    slots = jnp.max(pick_from(foot_tiles.reshape(-1), slot_of).reshape(NG, NC * FOOT), axis=1)
    return jnp.concatenate([rows, cen, picks, slots])


def body(traces, send_table, window_slots, ray_depth, ray_lateral, ray_spread, ray_index, foot_count, foot_tiles, tile_owner):
    group = lax.axis_index("beam")
    shot = lax.axis_index("shot")
    tab = scalar_table(group, shot, ray_index, foot_count, foot_tiles, tile_owner)
    send_col = lax.dynamic_index_in_dim(send_table[0], group, 0, keepdims=False).reshape(256, 1)
    win_col = window_slots[0].reshape(256, 1)
    return fused(tab, traces[0], send_col, win_col, ray_depth[0], ray_lateral, ray_spread)


def solution(mesh):
    in_specs = (
        P("shot", "beam", None),
        P("shot", None, None, None),
        P("shot", "beam", None),
        P("shot", "beam", None, None),
        P("beam", None, None),
        P("beam", None, None),
        P("beam", None),
        P("beam", None),
        P(),
        P(),
    )
    return jax.shard_map(body, mesh=mesh, in_specs=in_specs, out_specs=P(("shot", "beam"), None, None), check_vma=False)
```

time: 231 us -> 104 us (0.45)
  waiting for transfers between devices: 91.8 us -> 0 us
  Pallas kernels: 65.4 us -> 90.6 us
  matrix products: 18.3 us -> 0 us
  local copies, waits for them, and re-layouts: 22.1 us -> 6.58 us
  starting transfers between devices: 13.5 us -> 0 us
  between operations: 13.3 us -> 0.06 us
    all_gather x3 -> x0, waiting for transfers between devices: 66.9 us -> none  [the longest x1 43.4 us: body(): all_rows = lax.all_gather(traces[0], 'beam', axis=0, tiled=True)]
    pallas_call x1, Pallas kernels: 65.4 us -> 90.6 us  [fused(): pl.pallas_call(kernel, out_shape=jax.ShapeDtypeStruct((4, 128, 128), F32)...]
    all_to_all x2 -> x0, waiting for transfers between devices: 24.2 us -> none  [the longest x1 14.4 us: body(): lax.all_to_all(ray_depth[0][rows].reshape(8, NE, 32, 128), 'shot', 0, 1,...]
    dot_general x6 -> x0, matrix products: 18.3 us -> none  [the longest x4 14.7 us: es(): return jnp.einsum('fpk,ckf->cpf', a, b, preferred_element_type=jnp.float32)]
    gather x5 -> x0, local copies, waits for them, and re-layouts: 13.7 us -> none  [the longest x1 3.88 us: body(): ray_depth[0][rows].reshape(8, NE, 32, 128)]
    all_to_all x2 -> x0, starting transfers between devices: 13.4 us -> none  [the longest x1 6.71 us: body(): lax.all_to_all(ray_depth[0][rows].reshape(8, NE, 32, 128), 'shot', 0, 1,...]
  transfers between devices with their start and end apart: 5 -> 0, of which waited for: 4 -> 0; matrix products, arithmetic and copies ran while one was open for 8% -> 0% of each run, Pallas kernels for 0% -> 0%
where the time goes in v2:
time: 104 us; the launch traced here: 103 us
  Pallas kernels  90.6 us (87%)
  local copies, waits for them, and re-layouts  6.58 us (6%)
  other arithmetic  5.95 us (6%)
    pallas_call x1, Pallas kernels, fused(): pl.pallas_call(kernel, out_shape=jax.ShapeDtypeStruct((4, 128, 128), F32)...  90.6 us
    unnamed x4, local copies, waits for them, and re-layouts  2.48 us

profile of v2, /device:TPU:1, one launch (start us, length us, event | category | flops | bytes accessed | tf_op | source)
XLA Modules:
  0.0 103.2 jit_solution(2686390170013884666)
XLA Ops:
  0.0 0.0 copy-start
  0.0 0.8 select_reduce_fusion.6
  0.8 0.7 fusion.2
  1.5 0.1 convert_reduce_fusion.2
  1.6 0.1 select_reduce_fusion.5
  1.7 0.8 broadcast_in_dim.119
  2.4 0.7 broadcast_compare_fusion
  3.1 0.2 convert_reduce_fusion
  3.3 0.7 broadcast_select_fusion
  3.9 0.0 copy-done
  4.0 0.8 constant_dynamic-slice_fusion.1
  4.7 0.1 copy.18
  4.8 0.1 broadcast_in_dim.122
  4.9 0.2 select_reduce_fusion.4
  5.1 0.9 select_reduce_fusion.1
  5.9 0.2 convert_reduce_fusion.1
  6.1 0.1 select_reduce_fusion.2
  6.3 0.8 copy.19
  7.1 0.1 eq.108
  7.2 0.6 select_reduce_fusion
  7.8 0.1 reshape.43
  7.9 0.1 reduce_max.9
  8.0 0.7 pad_add_fusion.tab
  8.7 0.8 reshape.45.send_col
  9.4 1.5 %reshape_squeeze.4.win_col = s32[256,1]{1,0:T(8,128)} reshape(s32[1,8,32]{2,1,0:T(8,128)} %param.14) | data formatting | bytes 2048 | tf_op jit(solution)/shard_map/reshape;squeeze | solution.py:413
  10.9 90.6 %beam_migration.1 = f32[4,128,128]{2,1,0:T(8,128)} custom-call(s32[304]{0:T(512)} %pad_add_fusion.tab, bf16[256,128]{1,0:T(8,128)(2,1)} %bitcast.12, s32[256,1]{1,0:T(8,128)} %reshape.45.send_col, s32[256,1]{1,0:T(8,128)} %reshape_squeeze.4.win_col, bf16[32,32,128]{2,1,0:T(8,128)(2,1)} %constant.36.clone.t0, bf16[32,32,128]{2,1,0:T(8,128)(2,1)} %constant.37.clone.t1, ...), custom_call_target="tpu_custom_call" | custom-call | tf_op jit(solution)/shard_map/beam_migration/pallas_call | solution.py:354
  101.5 1.7 %copy.23 = f32[4,128,128]{2,1,0:T(8,128)} copy(f32[4,128,128]{2,1,0:T(8,128)} %beam_migration.1) | data formatting | bytes 524288
  (4 shorter events, 0.0 us)
Async XLA Ops:
  0.0 3.9 %copy-start = (s32[1,16,16,16]{3,2,1,0:T(8,128)S(1)}, s32[1,16,16,16]{3,2,1,0:T(8,128)}, u32[]{:S(2)}) copy-start(s32[1,16,16,16]{3,2,1,0:T(8,128)} %param.13) | copy-start | bytes 49156

commit v3 on v2

v3 whole, which is shorter than its diff:
```python
import math

import jax
import jax.numpy as jnp
import numpy as np
from jax import lax
from jax.experimental import pallas as pl
from jax.experimental.pallas import tpu as pltpu
from jax.sharding import PartitionSpec as P

MESH = pl.DeviceIdType.MESH
F32, BF16 = jnp.float32, jnp.bfloat16
NF, NP, NC, WIN, FOOT, LIVE = 64, 32, 8, 32, 12, 80
NS, NG, NE = 8, 16, 10
W0, DW, MID = 4.0, 60.0 / 64, 32
TWO_PI = 2.0 * math.pi
KP = 16
EARLY = 2
AT_ROW, AT_CEN, AT_PICK, AT_SLOT = 0, 1, 2, 3


def fit():
    x = np.cos(np.pi * (np.arange(400) + 0.5) / 400)
    q = (x * 0.5 + 0.5) * 0.25
    a = 2 * np.pi * np.sqrt(q)

    def poly(y, deg):
        c = np.polynomial.chebyshev.Chebyshev.fit(q, y, deg, domain=[0, 0.25])
        return [float(v) for v in c.convert(kind=np.polynomial.Polynomial).coef]

    return poly(np.cos(a), 7), poly(np.sin(a) / np.sqrt(q), 6)


COS_C, SIN_C = fit()


def sincos_turns(t):
    r = t - jnp.round(t)
    q = r * r
    cs = COS_C[-1]
    for c in COS_C[-2::-1]:
        cs = cs * q + c
    sn = SIN_C[-1]
    for c in SIN_C[-2::-1]:
        sn = sn * q + c
    return cs, sn * r


def stack_tables():
    f32 = np.float32
    angular = (2.0 * math.pi * (4.0 + 60.0 * np.arange(NF, dtype=f32) / NF)).astype(f32)
    centred = np.arange(WIN, dtype=f32) - f32(0.5 * (WIN - 1))
    taper = (np.exp(-((centred / f32(8.0)) ** 2)) / f32(math.sqrt(WIN))).astype(f32)
    slow = (f32(2e-05) * (np.arange(NP, dtype=f32) - f32(15.5))).astype(f32)
    angle = (angular[None, None, :] * slow[None, :, None]) * (f32(25.0) * centred)[:, None, None]
    sr = (taper[:, None, None] * np.cos(angle)).astype(BF16)
    si = (-taper[:, None, None] * np.sin(angle)).astype(BF16)
    return np.concatenate([sr, sr], 2), np.concatenate([-si, si], 2)


def lateral(tl, sp, l_scr, e):
    lc, ls = sincos_turns(W0 * tl)
    dm = jnp.exp(sp * (-TWO_PI * W0))
    lr, li = lc * dm, -(ls * dm)
    uc, us = sincos_turns(DW * tl)
    du = jnp.exp(sp * (-TWO_PI * DW))
    ur, ui = uc * du, -(us * du)
    for f in range(NF):
        l_scr[e, 0, f] = lr.astype(BF16)
        l_scr[e, 1, f] = li.astype(BF16)
        if f < NF - 1:
            lr, li = lr * ur - li * ui, lr * ui + li * ur


def depth_unit(c, d_scr, i, tdt, bt):
    z = pl.ds(pl.multiple_of(i * 16, 16), 16)
    seeds = []
    for h in range(2):
        t = tdt[h, z, :]
        c1, s1 = sincos_turns((W0 + DW * MID) * t)
        uc, us = sincos_turns(DW * t)
        seeds.append((c1 * uc + s1 * us, s1 * uc - c1 * us, c1, s1, uc + uc))

    def emit(f, st):
        ar = ai = None
        for h in range(2):
            br = bt[c, h, f : f + 1, :]
            bi = bt[c, h, NF + f : NF + f + 1, :]
            cv, sv = st[h][2], st[h][3]
            xr = br * cv - bi * sv
            xi = br * sv + bi * cv
            ar = xr if ar is None else ar + xr
            ai = xi if ai is None else ai + xi
        d_scr[f, 0, z, :] = ar.astype(BF16)
        d_scr[f, 1, z, :] = ai.astype(BF16)

    def step(st):
        return [(x[2], x[3], s[4] * x[2] - x[0], s[4] * x[3] - x[1]) for x, s in zip(st, seeds)]

    st = [s[:4] for s in seeds]
    for f in range(MID, NF):
        emit(f, st)
        if f < NF - 1:
            st = step(st)
    st = [(s[2], s[3], s[0], s[1]) for s in seeds]
    for f in range(MID - 1, -1, -1):
        emit(f, st)
        if f > 0:
            st = step(st)


def mm_piece(e, d_scr, i, l_scr, acc):
    part = i % 2
    f0 = (i // 2) * KP
    l8 = l_scr[e, part, pl.ds(f0, KP)]
    rhs = jnp.concatenate([l8[j] for j in range(KP) for _ in range(4)], 0)
    lhs = jnp.concatenate([d_scr[f0 + j, part] for j in range(KP)], 1)
    acc[...] += jnp.dot(lhs, rhs, preferred_element_type=F32)


def row_to_col(row):
    return jnp.broadcast_to(row, (128, 128)).T


def prep_kernel(count, index, foot, foot_v, owner_v, out_ref):
    shot = lax.axis_index("shot")
    beam = lax.axis_index("beam")
    n = lax.broadcasted_iota(jnp.int32, (1, 128), 1)
    cen = jnp.zeros((1, 128), jnp.int32)
    base = jnp.zeros((1, 128), jnp.int32)
    total = jnp.int32(0)
    for c in range(NC):
        prior = total
        total = total + count[0, c]
        cen = cen + jnp.where(n >= total, 1, 0)
        base = jnp.where(n >= prior, prior, base)
    eid = cen * FOOT + n - base
    rows = jnp.zeros((1, 128), jnp.int32)
    tile = jnp.zeros((1, 128), jnp.int32)
    for c in range(NC):
        for k in range(FOOT):
            hit = eid == c * FOOT + k
            rows = jnp.where(hit, index[c, k], rows)
            tile = jnp.where(hit, foot[beam * NC + c, k], tile)
    live = n < LIVE
    down = lax.broadcasted_iota(jnp.int32, (128, 128), 0).astype(F32)
    across = lax.broadcasted_iota(jnp.int32, (128, 128), 1).astype(F32)
    tile = tile.astype(F32)
    owners = owner_v[...].astype(F32)
    owner = jnp.zeros((1, 128), F32)
    for q in range(OWN_ROWS):
        hit = down + 128.0 * q == tile
        owner = owner + jnp.sum(jnp.where(hit, row_to_col(owners[q : q + 1]), 0.0), axis=0, keepdims=True)
    owner = jnp.where(live, owner, -1.0)
    same = (row_to_col(owner) == owner) & (down < across)
    rank = jnp.sum(jnp.where(same, 1.0, 0.0), axis=0, keepdims=True)
    key = jnp.where(live, (owner - (shot * NG).astype(F32)) * NC + rank, -1.0)
    hit = row_to_col(key) == across
    picks = LIVE + jnp.sum(jnp.where(hit, down - LIVE, 0.0), axis=0, keepdims=True)
    me = (shot * NG + beam).astype(F32)
    number = (
        lax.broadcasted_iota(jnp.int32, (OWN_ROWS, 128), 0) * 128 + lax.broadcasted_iota(jnp.int32, (OWN_ROWS, 128), 1)
    ).astype(F32)
    held = owners == me
    named = foot_v[...].astype(F32)
    slot = jnp.zeros(named.shape, F32)
    at = jnp.full((1, 1), -1.0, F32)
    for i in range(4):
        left = jnp.where(held & (number > at), number, 1e6)
        at = jnp.min(jnp.min(left, axis=0, keepdims=True), axis=1, keepdims=True)
        slot = jnp.where(named == at, float(i), slot)
    slot = jnp.max(slot, axis=1, keepdims=True)
    slot = jnp.broadcast_to(slot, (slot.shape[0], 128))
    if slot.shape[0] < 128:
        slot = jnp.concatenate([slot, jnp.zeros((128 - slot.shape[0], 128), F32)], 0)
    slot = slot.T[0:1]
    out_ref[...] = jnp.zeros((8, 128), jnp.int32)
    out_ref[AT_ROW : AT_ROW + 1] = rows
    out_ref[AT_CEN : AT_CEN + 1] = jnp.minimum(cen, NC - 1)
    out_ref[AT_PICK : AT_PICK + 1] = picks.astype(jnp.int32)
    out_ref[AT_SLOT : AT_SLOT + 1] = slot.astype(jnp.int32)


OWN_ROWS = NS * NG * 4 // 128


def prep(foot_count, ray_index, foot_tiles, tile_owner):
    vm, sm = pl.BlockSpec(memory_space=pltpu.VMEM), pl.BlockSpec(memory_space=pltpu.SMEM)
    return pl.pallas_call(
        prep_kernel,
        out_shape=jax.ShapeDtypeStruct((8, 128), jnp.int32),
        in_specs=[sm, sm, sm, vm, vm],
        out_specs=vm,
        name="entry_table",
    )(foot_count, ray_index, foot_tiles, foot_tiles, tile_owner.reshape(OWN_ROWS, 128))


def one_hot(x, count, width):
    xt = jnp.concatenate([x.astype(F32), jnp.zeros((x.shape[0], 128 - count), F32)], 1).T
    lanes = lax.broadcasted_iota(jnp.int32, (count, width), 1).astype(F32)
    parts = [jnp.where(lanes == xt[:count, r : r + 1], 1.0, 0.0) for r in range(x.shape[0])]
    return jnp.concatenate(parts, 0).astype(BF16)


def kernel(
    tab, traces, send_ref, win_ref, t0_hbm, t1_hbm, depth_hbm, lat_hbm, spr_hbm, out_ref,
    t0, t1, depth_v, lat_v, spr_v, tr_out, tr_in, win_s, win_r, ball, b_own, b_out, b_in, bt, td_out, td_in, tdt,
    d0, d1, l_scr, acc, tiles, dense, got,
    tab_sem, trs, trr, bs, br_sem, bes, ber, tds, tdr, tls, tlr, ows, owr,
):
    shot = lax.axis_index("shot")
    beam = lax.axis_index("beam")
    partner = shot + 1 - 2 * lax.rem(shot, 2)

    def at_shot(s):
        return dict(device_id={"shot": s, "beam": beam}, device_id_type=MESH)

    def at_beam(g):
        return dict(device_id={"shot": shot, "beam": g}, device_id_type=MESH)

    barrier = pltpu.get_barrier_semaphore()
    for d in range(1, NG):
        pl.semaphore_signal(barrier, inc=1, **at_beam(lax.rem(beam + d, NG)))
    for d in range(1, NS):
        pl.semaphore_signal(barrier, inc=1, **at_shot(lax.rem(shot + d, NS)))
    pairs = ((depth_hbm, depth_v), (lat_hbm, lat_v), (spr_hbm, spr_v), (t0_hbm, t0), (t1_hbm, t1))
    loads = [pltpu.make_async_copy(h, v, tab_sem.at[n]) for n, (h, v) in enumerate(pairs)]
    for cp in loads:
        cp.start()

    pick = one_hot(send_ref[beam], 16, 256)
    chosen = jnp.dot(pick, traces[...], preferred_element_type=F32).astype(BF16)
    tr_out[...] = chosen.reshape(NG, 16, 128)
    tr_in[beam] = tr_out[beam]
    pl.semaphore_wait(barrier, NS - 1 + NG - 1)

    def trace_copy(d):
        g = lax.rem(beam + d, NG)
        return pltpu.make_async_remote_copy(
            src_ref=tr_out.at[g], dst_ref=tr_in.at[beam], send_sem=trs.at[d], recv_sem=trr.at[d], **at_beam(g)
        )

    for d in range(1, NG):
        trace_copy(d).start()

    loads[0].wait()

    def gather(e, _):
        for j in range(NS):
            td_out[j, e] = depth_v[tab[AT_ROW, j * NE + e]]
        td_in[e, shot] = depth_v[tab[AT_ROW, shot * NE + e]]
        return 0

    lax.fori_loop(0, NE, gather, 0)

    def depth_copy(e, d):
        j = lax.rem(shot + d, NS)
        return pltpu.make_async_remote_copy(
            src_ref=td_out.at[j, e], dst_ref=td_in.at[e, shot], send_sem=tds.at[e, d], recv_sem=tdr.at[e, d], **at_shot(j)
        )

    for d in range(1, NS):
        depth_copy(0, d).start()
    loads[1].wait()
    loads[2].wait()

    def lat(e, _):
        r = tab[AT_ROW, shot * NE + e]
        lateral(lat_v[r], spr_v[r], l_scr, e)
        return 0

    lax.fori_loop(0, NE // 2, lat, 0)
    pick = one_hot(win_ref[...], WIN, NG * 16)
    loads[3].wait()
    loads[4].wait()

    for d in range(1, NG):
        trace_copy(d).wait_recv()
    win = jnp.dot(pick, tr_in[...].reshape(NG * 16, 128), preferred_element_type=F32)
    win_s[...] = win.reshape(NC, WIN, 128)
    win_r[...] = pltpu.roll(win, 64, 1).reshape(NC, WIN, 128)

    def stack(c, _):
        a = jnp.zeros((NP, 128), F32)
        for k in range(WIN):
            a = a + (t0[k].astype(F32) * win_s[c, k : k + 1, :] + t1[k].astype(F32) * win_r[c, k : k + 1, :])
        b_own[c] = a * (1.0 / math.sqrt(NP * NF))
        return 0

    lax.fori_loop(0, NC, stack, 0)

    def early_copy(e, d):
        j = lax.rem(shot + d, NS)
        return pltpu.make_async_remote_copy(
            src_ref=b_out.at[j, e], dst_ref=b_in.at[e, shot], send_sem=bes.at[e, d], recv_sem=ber.at[e, d], **at_shot(j)
        )

    for e in range(EARLY):
        for j in range(NS):
            b_out[j, e] = b_own[tab[AT_CEN, j * NE + e]]
        b_in[e, shot] = b_own[tab[AT_CEN, shot * NE + e]]
        for d in range(1, NS):
            early_copy(e, d).start()
        for d in range(1, NS):
            depth_copy(e + 1, d).start()

    def beam_copy(slot, n, to, own=True):
        return pltpu.make_async_remote_copy(
            src_ref=b_own if own else ball.at[slot], dst_ref=ball.at[slot], send_sem=bs.at[n], recv_sem=br_sem.at[n], **at_shot(to)
        )

    sends = [beam_copy(shot, 0, partner)]
    sends += [beam_copy(shot, d, lax.rem(shot + 2 * d, NS)) for d in range(1, 4)]
    for cp in sends:
        cp.start()

    def rest(e, _):
        for d in range(1, NS):
            depth_copy(e, d).start()
        return 0

    lax.fori_loop(EARLY + 1, NE, rest, 0)
    ball[shot] = b_own[...]
    lax.fori_loop(NE // 2, NE, lat, 0)

    def tile_copy(e, d):
        n = shot * NE + e
        return pltpu.make_async_remote_copy(
            src_ref=tiles.at[n], dst_ref=tiles.at[n], send_sem=tls.at[e, d], recv_sem=tlr.at[e, d],
            **at_shot(lax.rem(shot + d, NS)),
        )

    def share(e):
        tiles[shot * NE + e] = acc[...].astype(BF16)
        for d in range(1, NS):
            tile_copy(e, d).start()

    def both(e, c, dst, src):
        for d in range(1, NS):
            depth_copy(e, d).wait_recv()
        for h in range(2):
            tdt[h] = td_in[e, 4 * h : 4 * h + 4].reshape(128, 128).T
        acc[...] = jnp.zeros_like(acc)

        def unit(i, _):
            if src is not None:
                mm_piece(e - 1, src, i, l_scr, acc)
            depth_unit(c, dst, i, tdt, bt)
            return 0

        lax.fori_loop(0, 8, unit, 0)
        if src is not None:
            share(e - 1)

    def early(e):
        for d in range(1, NS):
            early_copy(e, d).wait_recv()
        for h in range(2):
            bt[NC + e, h] = b_in[e, 4 * h : 4 * h + 4].reshape(128, 128).T

    early(0)
    both(0, NC, d0, None)
    for d in range(1, 4):
        sends[d].wait_recv()
        cp = beam_copy(lax.rem(shot + NS - 2 * d, NS), 3 + d, partner, False)
        cp.start()
        sends.append(cp)
    early(1)
    both(1, NC + 1, d1, d0)
    for cp in sends[:1] + sends[4:]:
        cp.wait_recv()

    def turn(c, _):
        for h in range(2):
            bt[c, h] = jnp.concatenate([ball[4 * h + s, c] for s in range(4)], 0).T
        return 0

    lax.fori_loop(0, NC, turn, 0)

    def pair(k, _):
        both(2 * k, tab[AT_CEN, shot * NE + 2 * k], d0, d1)
        both(2 * k + 1, tab[AT_CEN, shot * NE + 2 * k + 1], d1, d0)
        return 0

    lax.fori_loop(1, NE // 2, pair, 0)
    acc[...] = jnp.zeros_like(acc)

    def last(i, _):
        mm_piece(NE - 1, d1, i, l_scr, acc)
        return 0

    lax.fori_loop(0, 8, last, 0)
    share(NE - 1)
    tiles[LIVE] = jnp.zeros((128, 128), BF16)

    def arrive(e, _):
        for d in range(1, NS):
            tile_copy(e, d).wait_recv()
        return 0

    lax.fori_loop(0, NE, arrive, 0)

    def owner_copy(d):
        g = lax.rem(beam + d, NG)
        return pltpu.make_async_remote_copy(
            src_ref=dense.at[g], dst_ref=got.at[beam], send_sem=ows.at[d], recv_sem=owr.at[d], **at_beam(g)
        )

    def gather_owner(d, _):
        g = lax.rem(beam + d, NG)
        s = tiles[tab[AT_PICK, g * NC]].astype(F32)
        for m in range(1, NC):
            s = s + tiles[tab[AT_PICK, g * NC + m]].astype(F32)
        dense[g] = s.astype(BF16)
        owner_copy(d).start()
        return 0

    lax.fori_loop(1, NG, gather_owner, 0)
    s = tiles[tab[AT_PICK, beam * NC]].astype(F32)
    for m in range(1, NC):
        s = s + tiles[tab[AT_PICK, beam * NC + m]].astype(F32)
    got[beam] = s.astype(BF16)

    for d in range(1, NG):
        trace_copy(d).wait_send()
    for cp in sends:
        cp.wait_send()

    def drain(e, _):
        for d in range(1, NS):
            depth_copy(e, d).wait_send()
            tile_copy(e, d).wait_send()
        return 0

    lax.fori_loop(0, NE, drain, 0)
    for e in range(EARLY):
        for d in range(1, NS):
            early_copy(e, d).wait_send()
    for slot in range(4):
        out_ref[slot] = jnp.zeros((128, 128), F32)

    for d in range(1, NG):
        owner_copy(d).wait_recv()

    def place(g, _):
        v = got[g].astype(F32)
        at = tab[AT_SLOT, g * NC]
        for c in range(1, NC):
            at = jnp.maximum(at, tab[AT_SLOT, g * NC + c])
        for slot in range(4):
            out_ref[slot] += v * jnp.where(at == slot, 1.0, 0.0)
        return 0

    lax.fori_loop(0, NG, place, 0)
    for d in range(1, NG):
        owner_copy(d).wait_send()


def fused(tab, traces, send, win, depth, lat, spr):
    t0, t1 = stack_tables()
    vm = pl.BlockSpec(memory_space=pltpu.VMEM)
    hbm = pl.BlockSpec(memory_space=pl.ANY)
    dma = pltpu.SemaphoreType.DMA
    return pl.pallas_call(
        kernel,
        out_shape=jax.ShapeDtypeStruct((4, 128, 128), F32),
        in_specs=[pl.BlockSpec(memory_space=pltpu.SMEM), vm, vm, vm, hbm, hbm, hbm, hbm, hbm],
        out_specs=vm,
        scratch_shapes=[
            pltpu.VMEM((WIN, NP, 128), BF16), pltpu.VMEM((WIN, NP, 128), BF16),
            pltpu.VMEM((256, 32, 128), F32), pltpu.VMEM((256, 32, 128), F32), pltpu.VMEM((256, 32, 128), F32),
            pltpu.VMEM((NG, 16, 128), BF16), pltpu.VMEM((NG, 16, 128), BF16),
            pltpu.VMEM((NC, WIN, 128), F32), pltpu.VMEM((NC, WIN, 128), F32),
            pltpu.VMEM((NS, NC, NP, 128), F32), pltpu.VMEM((NC, NP, 128), F32), pltpu.VMEM((NS, EARLY, NP, 128), F32), pltpu.VMEM((EARLY, NS, NP, 128), F32),
            pltpu.VMEM((NC + EARLY, 2, 128, 128), F32),
            pltpu.VMEM((NS, NE, NP, 128), F32), pltpu.VMEM((NE, NS, NP, 128), F32), pltpu.VMEM((2, 128, 128), F32),
            pltpu.VMEM((NF, 2, 128, 128), BF16), pltpu.VMEM((NF, 2, 128, 128), BF16),
            pltpu.VMEM((NE, 2, NF, NP, 128), BF16), pltpu.VMEM((128, 128), F32),
            pltpu.VMEM((LIVE + 1, 128, 128), BF16), pltpu.VMEM((NG, 128, 128), BF16), pltpu.VMEM((NG, 128, 128), BF16),
            dma((5,)), dma((NG,)), dma((NG,)), dma((7,)), dma((7,)), dma((EARLY, NS)), dma((EARLY, NS)),
            dma((NE, NS)), dma((NE, NS)), dma((NE, NS)), dma((NE, NS)), dma((NG,)), dma((NG,)),
        ],
        compiler_params=pltpu.CompilerParams(
            collective_id=0, has_side_effects=True, vmem_limit_bytes=62 * 1024 * 1024
        ),
        name="beam_migration",
    )(tab, traces, send, win, jnp.asarray(t0), jnp.asarray(t1), depth, lat, spr)


def body(traces, send_table, window_slots, ray_depth, ray_lateral, ray_spread, ray_index, foot_count, foot_tiles, tile_owner):
    tab = prep(foot_count, ray_index, foot_tiles, tile_owner)
    return fused(tab, traces[0], send_table[0], window_slots[0], ray_depth[0], ray_lateral, ray_spread)


def solution(mesh):
    in_specs = (
        P("shot", "beam", None),
        P("shot", None, None, None),
        P("shot", "beam", None),
        P("shot", "beam", None, None),
        P("beam", None, None),
        P("beam", None, None),
        P("beam", None),
        P("beam", None),
        P(),
        P(),
    )
    return jax.shard_map(body, mesh=mesh, in_specs=in_specs, out_specs=P(("shot", "beam"), None, None), check_vma=False)
```

time: 104 us -> 96 us (0.923)
  other arithmetic: 5.95 us -> 0 us
  local copies, waits for them, and re-layouts: 6.58 us -> 3.1 us
  Pallas kernels: 90.6 us -> 92.6 us
    reduce_sum x9 -> x0, other arithmetic: 3.12 us -> none  [the longest x4 1.78 us: pick_from(): return jnp.sum(jnp.where(hit, table[None, :], 0), axis=1)]
    pallas_call x0 -> x1, Pallas kernels: none -> 2.98 us  [prep(): pl.pallas_call(prep_kernel, out_shape=jax.ShapeDtypeStruct((8, 128), jnp....]
    another operation x1 -> x0, local copies, waits for them, and re-layouts: 1.48 us -> none  [body(): win_col = window_slots[0].reshape(256, 1)]
    unnamed x4 -> x2, local copies, waits for them, and re-layouts: 2.48 us -> 3.1 us
where the time goes in v3:
time: 96 us; the launch traced here: 95.7 us
  Pallas kernels  92.6 us (96%)
  local copies, waits for them, and re-layouts  3.1 us (3%)
    pallas_call x1, Pallas kernels, fused(): pl.pallas_call(kernel, out_shape=jax.ShapeDtypeStruct((4, 128, 128), F32)...  89.7 us
    unnamed x2, local copies, waits for them, and re-layouts  3.1 us
    pallas_call x1, Pallas kernels, prep(): pl.pallas_call(prep_kernel, out_shape=jax.ShapeDtypeStruct((8, 128), jnp....  2.98 us

profile of v3, /device:TPU:1, one launch (start us, length us, event | category | flops | bytes accessed | tf_op | source)
XLA Modules:
  0.0 95.7 jit_solution(10126725712486288538)
XLA Ops:
  0.0 1.4 %copy.13.foot.foot_v = s32[128,12]{1,0:T(8,128)} copy(s32[128,12]{0,1:T(8,128)} %param.20) | data formatting | bytes 12288 | tf_op args[8]
  1.4 3.0 %entry_table.1.tab = s32[8,128]{1,0:T(8,128)} custom-call(s32[1,8]{1,0:T(1,128)} %count.1, s32[8,12]{1,0:T(8,128)} %index.1, s32[128,12]{1,0:T(8,128)} %copy.13.foot.foot_v, s32[128,12]{1,0:T(8,128)} %copy.13.foot.foot_v, s32[4,128]{1,0:T(4,128)} %bitcast.9), custom_call_target="tpu_custom_call" | custom-call | tf_op jit(solution)/shard_map/entry_table/pallas_call | solution.py:189
  4.4 89.7 %beam_migration.1 = f32[4,128,128]{2,1,0:T(8,128)} custom-call(s32[8,128]{1,0:T(8,128)} %entry_table.1.tab, bf16[256,128]{1,0:T(8,128)(2,1)} %bitcast.7, s32[16,16,16]{2,1,0:T(8,128)} %bitcast.6, s32[8,32]{1,0:T(8,128)} %bitcast.8, bf16[32,32,128]{2,1,0:T(8,128)(2,1)} %constant.4.clone.t0_hbm, bf16[32,32,128]{2,1,0:T(8,128)(2,1)} %constant.5.clone.t1_hbm, ...), custom_call_target="tpu_custom_call" | custom-call | tf_op jit(solution)/shard_map/beam_migration/pallas_call | solution.py:464
  94.1 1.7 %copy.16 = f32[4,128,128]{2,1,0:T(8,128)} copy(f32[4,128,128]{2,1,0:T(8,128)} %beam_migration.1) | data formatting | bytes 524288

commit v4 on v3

--- a/solution.py
+++ b/solution.py
@@ -210,13 +210,23 @@
 ):
     shot = lax.axis_index("shot")
     beam = lax.axis_index("beam")
-    partner = shot + 1 - 2 * lax.rem(shot, 2)
+    way = 1 - 2 * lax.rem(shot, 2)
+    partner = shot + way
+    ahead = lax.rem(shot + 2 * way + NS, NS)
+    behind = lax.rem(shot - 2 * way + NS, NS)
+    ring = (
+        (shot, ahead), (shot, behind), (shot, partner),
+        (behind, ahead), (behind, ahead + way), (behind, partner), (ahead, partner),
+    )
 
     def at_shot(s):
         return dict(device_id={"shot": s, "beam": beam}, device_id_type=MESH)
 
     def at_beam(g):
         return dict(device_id={"shot": shot, "beam": g}, device_id_type=MESH)
+
+    def await_all(ref, sem):
+        pltpu.make_async_copy(ref, ref, sem).wait()
 
     barrier = pltpu.get_barrier_semaphore()
     for d in range(1, NG):
@@ -237,7 +247,7 @@
     def trace_copy(d):
         g = lax.rem(beam + d, NG)
         return pltpu.make_async_remote_copy(
-            src_ref=tr_out.at[g], dst_ref=tr_in.at[beam], send_sem=trs.at[d], recv_sem=trr.at[d], **at_beam(g)
+            src_ref=tr_out.at[g], dst_ref=tr_in.at[beam], send_sem=trs, recv_sem=trr, **at_beam(g)
         )
 
     for d in range(1, NG):
@@ -256,7 +266,7 @@
     def depth_copy(e, d):
         j = lax.rem(shot + d, NS)
         return pltpu.make_async_remote_copy(
-            src_ref=td_out.at[j, e], dst_ref=td_in.at[e, shot], send_sem=tds.at[e, d], recv_sem=tdr.at[e, d], **at_shot(j)
+            src_ref=td_out.at[j, e], dst_ref=td_in.at[e, shot], send_sem=tds, recv_sem=tdr.at[e], **at_shot(j)
         )
 
     for d in range(1, NS):
@@ -274,8 +284,7 @@
     loads[3].wait()
     loads[4].wait()
 
-    for d in range(1, NG):
-        trace_copy(d).wait_recv()
+    await_all(tr_in.at[0 : NG - 1], trr)
     win = jnp.dot(pick, tr_in[...].reshape(NG * 16, 128), preferred_element_type=F32)
     win_s[...] = win.reshape(NC, WIN, 128)
     win_r[...] = pltpu.roll(win, 64, 1).reshape(NC, WIN, 128)
@@ -292,52 +301,51 @@
     def early_copy(e, d):
         j = lax.rem(shot + d, NS)
         return pltpu.make_async_remote_copy(
-            src_ref=b_out.at[j, e], dst_ref=b_in.at[e, shot], send_sem=bes.at[e, d], recv_sem=ber.at[e, d], **at_shot(j)
+            src_ref=b_out.at[j, e], dst_ref=b_in.at[e, shot], send_sem=bes, recv_sem=ber.at[e], **at_shot(j)
         )
 
     for e in range(EARLY):
         for j in range(NS):
             b_out[j, e] = b_own[tab[AT_CEN, j * NE + e]]
         b_in[e, shot] = b_own[tab[AT_CEN, shot * NE + e]]
-        for d in range(1, NS):
-            early_copy(e, d).start()
-        for d in range(1, NS):
-            depth_copy(e + 1, d).start()
-
-    def beam_copy(slot, n, to, own=True):
+
+    def beam_copy(n):
+        item, to = ring[n]
         return pltpu.make_async_remote_copy(
-            src_ref=b_own if own else ball.at[slot], dst_ref=ball.at[slot], send_sem=bs.at[n], recv_sem=br_sem.at[n], **at_shot(to)
+            src_ref=b_own if n < 3 else ball.at[item], dst_ref=ball.at[item],
+            send_sem=bs.at[n], recv_sem=br_sem.at[n], **at_shot(to),
         )
-
-    sends = [beam_copy(shot, 0, partner)]
-    sends += [beam_copy(shot, d, lax.rem(shot + 2 * d, NS)) for d in range(1, 4)]
-    for cp in sends:
-        cp.start()
-
-    def rest(e, _):
-        for d in range(1, NS):
-            depth_copy(e, d).start()
-        return 0
-
-    lax.fori_loop(EARLY + 1, NE, rest, 0)
-    ball[shot] = b_own[...]
-    lax.fori_loop(NE // 2, NE, lat, 0)
 
     def tile_copy(e, d):
         n = shot * NE + e
         return pltpu.make_async_remote_copy(
-            src_ref=tiles.at[n], dst_ref=tiles.at[n], send_sem=tls.at[e, d], recv_sem=tlr.at[e, d],
-            **at_shot(lax.rem(shot + d, NS)),
+            src_ref=tiles.at[n], dst_ref=tiles.at[n], send_sem=tls, recv_sem=tlr, **at_shot(lax.rem(shot + d, NS))
         )
+
+    def early_send(e):
+        for d in range(1, NS):
+            early_copy(e, d).start()
+
+    def depth_send(e):
+        for d in range(1, NS):
+            depth_copy(e, d).start()
+
+    early_send(0)
+    for n in range(3):
+        beam_copy(n).start()
+    depth_send(1)
+    for e in range(1, EARLY):
+        early_send(e)
+    ball[shot] = b_own[...]
+    lax.fori_loop(NE // 2, NE, lat, 0)
 
     def share(e):
         tiles[shot * NE + e] = acc[...].astype(BF16)
         for d in range(1, NS):
             tile_copy(e, d).start()
 
-    def both(e, c, dst, src):
-        for d in range(1, NS):
-            depth_copy(e, d).wait_recv()
+    def both(e, c, dst, src, after=None):
+        await_all(td_in.at[e, 0 : NS - 1], tdr.at[e])
         for h in range(2):
             tdt[h] = td_in[e, 4 * h : 4 * h + 4].reshape(128, 128).T
         acc[...] = jnp.zeros_like(acc)
@@ -351,24 +359,33 @@
         lax.fori_loop(0, 8, unit, 0)
         if src is not None:
             share(e - 1)
+        if after is not None:
+            after()
+        if isinstance(e, int):
+            depth_send(e + 2)
+        else:
+
+            @pl.when(e + 2 < NE)
+            def _():
+                depth_send(e + 2)
 
     def early(e):
-        for d in range(1, NS):
-            early_copy(e, d).wait_recv()
+        await_all(b_in.at[e, 0 : NS - 1], ber.at[e])
         for h in range(2):
             bt[NC + e, h] = b_in[e, 4 * h : 4 * h + 4].reshape(128, 128).T
 
+    def pass_beams():
+        for n in range(2):
+            beam_copy(n).wait_recv()
+        for n in range(3, 7):
+            beam_copy(n).start()
+
     early(0)
-    both(0, NC, d0, None)
-    for d in range(1, 4):
-        sends[d].wait_recv()
-        cp = beam_copy(lax.rem(shot + NS - 2 * d, NS), 3 + d, partner, False)
-        cp.start()
-        sends.append(cp)
+    both(0, NC, d0, None, pass_beams)
     early(1)
     both(1, NC + 1, d1, d0)
-    for cp in sends[:1] + sends[4:]:
-        cp.wait_recv()
+    for n in range(2, 7):
+        beam_copy(n).wait_recv()
 
     def turn(c, _):
         for h in range(2):
@@ -393,17 +410,12 @@
     share(NE - 1)
     tiles[LIVE] = jnp.zeros((128, 128), BF16)
 
-    def arrive(e, _):
-        for d in range(1, NS):
-            tile_copy(e, d).wait_recv()
-        return 0
-
-    lax.fori_loop(0, NE, arrive, 0)
+    await_all(tiles.at[0 : LIVE - NE], tlr)
 
     def owner_copy(d):
         g = lax.rem(beam + d, NG)
         return pltpu.make_async_remote_copy(
-            src_ref=dense.at[g], dst_ref=got.at[beam], send_sem=ows.at[d], recv_sem=owr.at[d], **at_beam(g)
+            src_ref=dense.at[g], dst_ref=got.at[beam], send_sem=ows, recv_sem=owr, **at_beam(g)
         )
 
     def gather_owner(d, _):
@@ -421,26 +433,17 @@
         s = s + tiles[tab[AT_PICK, beam * NC + m]].astype(F32)
     got[beam] = s.astype(BF16)
 
-    for d in range(1, NG):
-        trace_copy(d).wait_send()
-    for cp in sends:
-        cp.wait_send()
-
-    def drain(e, _):
-        for d in range(1, NS):
-            depth_copy(e, d).wait_send()
-            tile_copy(e, d).wait_send()
-        return 0
-
-    lax.fori_loop(0, NE, drain, 0)
-    for e in range(EARLY):
-        for d in range(1, NS):
-            early_copy(e, d).wait_send()
+    await_all(tr_out.at[0 : NG - 1], trs)
+    for n in range(7):
+        beam_copy(n).wait_send()
+
+    await_all(td_out.at[0 : NS - 1], tds)
+    await_all(tiles.at[0 : LIVE - NE], tls)
+    await_all(b_out.at[0 : NS - 1], bes)
     for slot in range(4):
         out_ref[slot] = jnp.zeros((128, 128), F32)
 
-    for d in range(1, NG):
-        owner_copy(d).wait_recv()
+    await_all(got.at[0 : NG - 1], owr)
 
     def place(g, _):
         v = got[g].astype(F32)
@@ -452,8 +455,7 @@
         return 0
 
     lax.fori_loop(0, NG, place, 0)
-    for d in range(1, NG):
-        owner_copy(d).wait_send()
+    await_all(dense.at[0 : NG - 1], ows)
 
 
 def fused(tab, traces, send, win, depth, lat, spr):
@@ -477,8 +479,8 @@
             pltpu.VMEM((NF, 2, 128, 128), BF16), pltpu.VMEM((NF, 2, 128, 128), BF16),
             pltpu.VMEM((NE, 2, NF, NP, 128), BF16), pltpu.VMEM((128, 128), F32),
             pltpu.VMEM((LIVE + 1, 128, 128), BF16), pltpu.VMEM((NG, 128, 128), BF16), pltpu.VMEM((NG, 128, 128), BF16),
-            dma((5,)), dma((NG,)), dma((NG,)), dma((7,)), dma((7,)), dma((EARLY, NS)), dma((EARLY, NS)),
-            dma((NE, NS)), dma((NE, NS)), dma((NE, NS)), dma((NE, NS)), dma((NG,)), dma((NG,)),
+            dma((5,)), dma(()), dma(()), dma((7,)), dma((7,)), dma(()), dma((EARLY,)),
+            dma(()), dma((NE,)), dma(()), dma(()), dma(()), dma(()),
         ],
         compiler_params=pltpu.CompilerParams(
             collective_id=0, has_side_effects=True, vmem_limit_bytes=62 * 1024 * 1024

time: 96 us -> 97.3 us (1.014)
  Pallas kernels: 92.6 us -> 93.9 us
    pallas_call x1, Pallas kernels: 89.7 us -> 91 us  [fused(): pl.pallas_call(kernel, out_shape=jax.ShapeDtypeStruct((4, 128, 128), F32)...]
where the time goes in v4:
time: 97.3 us; the launch traced here: 97 us
  Pallas kernels  93.9 us (97%)
  local copies, waits for them, and re-layouts  3.1 us (3%)
    pallas_call x1, Pallas kernels, fused(): pl.pallas_call(kernel, out_shape=jax.ShapeDtypeStruct((4, 128, 128), F32)...  91 us
    unnamed x2, local copies, waits for them, and re-layouts  3.1 us
    pallas_call x1, Pallas kernels, prep(): pl.pallas_call(prep_kernel, out_shape=jax.ShapeDtypeStruct((8, 128), jnp....  2.98 us

profile of v4, /device:TPU:1, one launch (start us, length us, event | category | flops | bytes accessed | tf_op | source)
XLA Modules:
  0.0 97.0 jit_solution(3126701745445087426)
XLA Ops:
  0.0 1.4 %copy.13.foot.foot_v = s32[128,12]{1,0:T(8,128)} copy(s32[128,12]{0,1:T(8,128)} %param.20) | data formatting | bytes 12288 | tf_op args[8]
  1.4 3.0 %entry_table.1.tab = s32[8,128]{1,0:T(8,128)} custom-call(s32[1,8]{1,0:T(1,128)} %count.1, s32[8,12]{1,0:T(8,128)} %index.1, s32[128,12]{1,0:T(8,128)} %copy.13.foot.foot_v, s32[128,12]{1,0:T(8,128)} %copy.13.foot.foot_v, s32[4,128]{1,0:T(4,128)} %bitcast.9), custom_call_target="tpu_custom_call" | custom-call | tf_op jit(solution)/shard_map/entry_table/pallas_call | solution.py:189
  4.4 91.0 %beam_migration.1 = f32[4,128,128]{2,1,0:T(8,128)} custom-call(s32[8,128]{1,0:T(8,128)} %entry_table.1.tab, bf16[256,128]{1,0:T(8,128)(2,1)} %bitcast.7, s32[16,16,16]{2,1,0:T(8,128)} %bitcast.6, s32[8,32]{1,0:T(8,128)} %bitcast.8, bf16[32,32,128]{2,1,0:T(8,128)(2,1)} %constant.4.clone.t0_hbm, bf16[32,32,128]{2,1,0:T(8,128)(2,1)} %constant.5.clone.t1_hbm, ...), custom_call_target="tpu_custom_call" | custom-call | tf_op jit(solution)/shard_map/beam_migration/pallas_call | solution.py:466
  95.4 1.7 %copy.16 = f32[4,128,128]{2,1,0:T(8,128)} copy(f32[4,128,128]{2,1,0:T(8,128)} %beam_migration.1) | data formatting | bytes 524288

commit v5 on v4

--- a/solution.py
+++ b/solution.py
@@ -1,3 +1,4 @@
+import functools
 import math
 
 import jax
@@ -109,13 +110,23 @@
             st = step(st)
 
 
-def mm_piece(e, d_scr, i, l_scr, acc):
+def mm_piece(e, d_scr, i, l_scr, accs):
     part = i % 2
     f0 = (i // 2) * KP
-    l8 = l_scr[e, part, pl.ds(f0, KP)]
-    rhs = jnp.concatenate([l8[j] for j in range(KP) for _ in range(4)], 0)
-    lhs = jnp.concatenate([d_scr[f0 + j, part] for j in range(KP)], 1)
-    acc[...] += jnp.dot(lhs, rhs, preferred_element_type=F32)
+    blank = jnp.zeros((256, 128), BF16)
+    for t in range(KP // 2):
+        unit = t % 2
+        f = f0 + 2 * t
+        la, lb = l_scr[e, part, f], l_scr[e, part, f + 1]
+        rhs = jnp.concatenate([jnp.concatenate([la] * 4 + [lb] * 4, 0), blank], 1)
+        stage = (t // 2) % 2
+        pltpu.matmul_push_rhs(rhs, stage, unit)
+        lhs = jnp.concatenate([d_scr[f, part], d_scr[f + 1, part]], 1)
+        pltpu.matmul_acc_lhs(accs[unit], lhs, load_staged_rhs=stage)
+
+
+def mm_result(accs):
+    return pltpu.matmul_pop(accs[0])[:, :128] + pltpu.matmul_pop(accs[1])[:, :128]
 
 
 def row_to_col(row):
@@ -141,7 +152,7 @@
         for k in range(FOOT):
             hit = eid == c * FOOT + k
             rows = jnp.where(hit, index[c, k], rows)
-            tile = jnp.where(hit, foot[beam * NC + c, k], tile)
+            tile = jnp.where(hit, foot[k, beam * NC + c], tile)
     live = n < LIVE
     down = lax.broadcasted_iota(jnp.int32, (128, 128), 0).astype(F32)
     across = lax.broadcasted_iota(jnp.int32, (128, 128), 1).astype(F32)
@@ -169,11 +180,7 @@
         left = jnp.where(held & (number > at), number, 1e6)
         at = jnp.min(jnp.min(left, axis=0, keepdims=True), axis=1, keepdims=True)
         slot = jnp.where(named == at, float(i), slot)
-    slot = jnp.max(slot, axis=1, keepdims=True)
-    slot = jnp.broadcast_to(slot, (slot.shape[0], 128))
-    if slot.shape[0] < 128:
-        slot = jnp.concatenate([slot, jnp.zeros((128 - slot.shape[0], 128), F32)], 0)
-    slot = slot.T[0:1]
+    slot = jnp.max(slot, axis=0, keepdims=True)
     out_ref[...] = jnp.zeros((8, 128), jnp.int32)
     out_ref[AT_ROW : AT_ROW + 1] = rows
     out_ref[AT_CEN : AT_CEN + 1] = jnp.minimum(cen, NC - 1)
@@ -192,7 +199,7 @@
         in_specs=[sm, sm, sm, vm, vm],
         out_specs=vm,
         name="entry_table",
-    )(foot_count, ray_index, foot_tiles, foot_tiles, tile_owner.reshape(OWN_ROWS, 128))
+    )(foot_count, ray_index, foot_tiles.T, foot_tiles.T, tile_owner.reshape(OWN_ROWS, 128))
 
 
 def one_hot(x, count, width):
@@ -203,10 +210,10 @@
 
 
 def kernel(
-    tab, traces, send_ref, win_ref, t0_hbm, t1_hbm, depth_hbm, lat_hbm, spr_hbm, out_ref,
+    mesh, tab, traces, send_ref, win_ref, t0_hbm, t1_hbm, depth_hbm, lat_hbm, spr_hbm, out_ref,
     t0, t1, depth_v, lat_v, spr_v, tr_out, tr_in, win_s, win_r, ball, b_own, b_out, b_in, bt, td_out, td_in, tdt,
-    d0, d1, l_scr, acc, tiles, dense, got,
-    tab_sem, trs, trr, bs, br_sem, bes, ber, tds, tdr, tls, tlr, ows, owr,
+    d0, d1, l_scr, tiles, dense, got,
+    tab_sem, trs, trr, bs, br_sem, bes, ber, tds, tdr, tls, tln, tlr, ows, owr,
 ):
     shot = lax.axis_index("shot")
     beam = lax.axis_index("beam")
@@ -238,8 +245,19 @@
     for cp in loads:
         cp.start()
 
+    def select(pick, rows):
+        def go(total):
+            wide = jnp.concatenate([rows, jnp.zeros((256, 128), BF16)], 1)
+            pltpu.matmul_push_rhs(wide, 0, 0)
+            pltpu.matmul_acc_lhs(total, pick, load_staged_rhs=0)
+            return pltpu.matmul_pop(total)[:, :128]
+
+        with jax.sharding.use_abstract_mesh(mesh.abstract_mesh):
+            kind = pltpu.ACC(0)((256, 256), F32)
+        return pl.run_scoped(go, kind)
+
     pick = one_hot(send_ref[beam], 16, 256)
-    chosen = jnp.dot(pick, traces[...], preferred_element_type=F32).astype(BF16)
+    chosen = select(pick, traces[...]).astype(BF16)
     tr_out[...] = chosen.reshape(NG, 16, 128)
     tr_in[beam] = tr_out[beam]
     pl.semaphore_wait(barrier, NS - 1 + NG - 1)
@@ -285,7 +303,7 @@
     loads[4].wait()
 
     await_all(tr_in.at[0 : NG - 1], trr)
-    win = jnp.dot(pick, tr_in[...].reshape(NG * 16, 128), preferred_element_type=F32)
+    win = select(pick, tr_in[...].reshape(NG * 16, 128))
     win_s[...] = win.reshape(NC, WIN, 128)
     win_r[...] = pltpu.roll(win, 64, 1).reshape(NC, WIN, 128)
 
@@ -316,11 +334,17 @@
             send_sem=bs.at[n], recv_sem=br_sem.at[n], **at_shot(to),
         )
 
-    def tile_copy(e, d):
-        n = shot * NE + e
+    def tile_copy(e, n):
+        item, to = ring[n]
         return pltpu.make_async_remote_copy(
-            src_ref=tiles.at[n], dst_ref=tiles.at[n], send_sem=tls, recv_sem=tlr, **at_shot(lax.rem(shot + d, NS))
+            src_ref=tiles.at[item * NE + e], dst_ref=tiles.at[item * NE + e],
+            send_sem=tls, recv_sem=tln.at[e] if n < 2 else tlr, **at_shot(to),
         )
+
+    def relay(e):
+        await_all(tiles.at[0:2], tln.at[e])
+        for n in range(3, 7):
+            tile_copy(e, n).start()
 
     def early_send(e):
         for d in range(1, NS):
@@ -339,31 +363,31 @@
     ball[shot] = b_own[...]
     lax.fori_loop(NE // 2, NE, lat, 0)
 
-    def share(e):
-        tiles[shot * NE + e] = acc[...].astype(BF16)
-        for d in range(1, NS):
-            tile_copy(e, d).start()
-
-    def both(e, c, dst, src, after=None):
+    def share(e, accs):
+        tiles[shot * NE + e] = mm_result(accs).astype(BF16)
+        for n in range(3):
+            tile_copy(e, n).start()
+
+    def both(accs, e, c, dst, src, after=None):
         await_all(td_in.at[e, 0 : NS - 1], tdr.at[e])
         for h in range(2):
             tdt[h] = td_in[e, 4 * h : 4 * h + 4].reshape(128, 128).T
-        acc[...] = jnp.zeros_like(acc)
 
         def unit(i, _):
             if src is not None:
-                mm_piece(e - 1, src, i, l_scr, acc)
+                mm_piece(e - 1, src, i, l_scr, accs)
             depth_unit(c, dst, i, tdt, bt)
             return 0
 
         lax.fori_loop(0, 8, unit, 0)
         if src is not None:
-            share(e - 1)
+            share(e - 1, accs)
         if after is not None:
             after()
         if isinstance(e, int):
             depth_send(e + 2)
         else:
+            relay(e - 2)
 
             @pl.when(e + 2 < NE)
             def _():
@@ -380,37 +404,43 @@
         for n in range(3, 7):
             beam_copy(n).start()
 
-    early(0)
-    both(0, NC, d0, None, pass_beams)
-    early(1)
-    both(1, NC + 1, d1, d0)
-    for n in range(2, 7):
-        beam_copy(n).wait_recv()
-
-    def turn(c, _):
-        for h in range(2):
-            bt[c, h] = jnp.concatenate([ball[4 * h + s, c] for s in range(4)], 0).T
-        return 0
-
-    lax.fori_loop(0, NC, turn, 0)
-
-    def pair(k, _):
-        both(2 * k, tab[AT_CEN, shot * NE + 2 * k], d0, d1)
-        both(2 * k + 1, tab[AT_CEN, shot * NE + 2 * k + 1], d1, d0)
-        return 0
-
-    lax.fori_loop(1, NE // 2, pair, 0)
-    acc[...] = jnp.zeros_like(acc)
-
-    def last(i, _):
-        mm_piece(NE - 1, d1, i, l_scr, acc)
-        return 0
-
-    lax.fori_loop(0, 8, last, 0)
-    share(NE - 1)
+    def migrate(*accs):
+        early(0)
+        both(accs, 0, NC, d0, None, pass_beams)
+        early(1)
+        both(accs, 1, NC + 1, d1, d0)
+        for n in range(2, 7):
+            beam_copy(n).wait_recv()
+
+        def turn(c, _):
+            for h in range(2):
+                bt[c, h] = jnp.concatenate([ball[4 * h + s, c] for s in range(4)], 0).T
+            return 0
+
+        lax.fori_loop(0, NC, turn, 0)
+
+        def pair(k, _):
+            both(accs, 2 * k, tab[AT_CEN, shot * NE + 2 * k], d0, d1)
+            both(accs, 2 * k + 1, tab[AT_CEN, shot * NE + 2 * k + 1], d1, d0)
+            return 0
+
+        lax.fori_loop(1, NE // 2, pair, 0)
+
+        def last(i, _):
+            mm_piece(NE - 1, d1, i, l_scr, accs)
+            return 0
+
+        lax.fori_loop(0, 8, last, 0)
+        share(NE - 1, accs)
+
+    with jax.sharding.use_abstract_mesh(mesh.abstract_mesh):
+        kinds = [pltpu.ACC(u)((128, 256), F32) for u in range(2)]
+    pl.run_scoped(migrate, *kinds)
+    relay(NE - 2)
     tiles[LIVE] = jnp.zeros((128, 128), BF16)
-
-    await_all(tiles.at[0 : LIVE - NE], tlr)
+    relay(NE - 1)
+
+    await_all(tiles.at[0 : 5 * NE], tlr)
 
     def owner_copy(d):
         g = lax.rem(beam + d, NG)
@@ -440,31 +470,36 @@
     await_all(td_out.at[0 : NS - 1], tds)
     await_all(tiles.at[0 : LIVE - NE], tls)
     await_all(b_out.at[0 : NS - 1], bes)
-    for slot in range(4):
-        out_ref[slot] = jnp.zeros((128, 128), F32)
-
     await_all(got.at[0 : NG - 1], owr)
 
-    def place(g, _):
-        v = got[g].astype(F32)
+    weights = []
+    for g in range(NG):
         at = tab[AT_SLOT, g * NC]
         for c in range(1, NC):
             at = jnp.maximum(at, tab[AT_SLOT, g * NC + c])
+        weights.append([jnp.where(at == slot, 1.0, 0.0) for slot in range(4)])
+
+    def place(i, _):
+        z = pl.ds(pl.multiple_of(i * 16, 16), 16)
+        sums = [jnp.zeros((16, 128), F32)] * 4
+        for g in range(NG):
+            v = got[g, z, :].astype(F32)
+            sums = [a + v * w for a, w in zip(sums, weights[g])]
         for slot in range(4):
-            out_ref[slot] += v * jnp.where(at == slot, 1.0, 0.0)
+            out_ref[slot, z, :] = sums[slot]
         return 0
 
-    lax.fori_loop(0, NG, place, 0)
+    lax.fori_loop(0, 8, place, 0)
     await_all(dense.at[0 : NG - 1], ows)
 
 
-def fused(tab, traces, send, win, depth, lat, spr):
+def fused(mesh, tab, traces, send, win, depth, lat, spr):
     t0, t1 = stack_tables()
     vm = pl.BlockSpec(memory_space=pltpu.VMEM)
     hbm = pl.BlockSpec(memory_space=pl.ANY)
     dma = pltpu.SemaphoreType.DMA
     return pl.pallas_call(
-        kernel,
+        functools.partial(kernel, mesh),
         out_shape=jax.ShapeDtypeStruct((4, 128, 128), F32),
         in_specs=[pl.BlockSpec(memory_space=pltpu.SMEM), vm, vm, vm, hbm, hbm, hbm, hbm, hbm],
         out_specs=vm,
@@ -477,10 +512,10 @@
             pltpu.VMEM((NC + EARLY, 2, 128, 128), F32),
             pltpu.VMEM((NS, NE, NP, 128), F32), pltpu.VMEM((NE, NS, NP, 128), F32), pltpu.VMEM((2, 128, 128), F32),
             pltpu.VMEM((NF, 2, 128, 128), BF16), pltpu.VMEM((NF, 2, 128, 128), BF16),
-            pltpu.VMEM((NE, 2, NF, NP, 128), BF16), pltpu.VMEM((128, 128), F32),
+            pltpu.VMEM((NE, 2, NF, NP, 128), BF16),
             pltpu.VMEM((LIVE + 1, 128, 128), BF16), pltpu.VMEM((NG, 128, 128), BF16), pltpu.VMEM((NG, 128, 128), BF16),
             dma((5,)), dma(()), dma(()), dma((7,)), dma((7,)), dma(()), dma((EARLY,)),
-            dma(()), dma((NE,)), dma(()), dma(()), dma(()), dma(()),
+            dma(()), dma((NE,)), dma(()), dma((NE,)), dma(()), dma(()), dma(()),
         ],
         compiler_params=pltpu.CompilerParams(
             collective_id=0, has_side_effects=True, vmem_limit_bytes=62 * 1024 * 1024
@@ -489,9 +524,9 @@
     )(tab, traces, send, win, jnp.asarray(t0), jnp.asarray(t1), depth, lat, spr)
 
 
-def body(traces, send_table, window_slots, ray_depth, ray_lateral, ray_spread, ray_index, foot_count, foot_tiles, tile_owner):
+def body(mesh, traces, send_table, window_slots, ray_depth, ray_lateral, ray_spread, ray_index, foot_count, foot_tiles, tile_owner):
     tab = prep(foot_count, ray_index, foot_tiles, tile_owner)
-    return fused(tab, traces[0], send_table[0], window_slots[0], ray_depth[0], ray_lateral, ray_spread)
+    return fused(mesh, tab, traces[0], send_table[0], window_slots[0], ray_depth[0], ray_lateral, ray_spread)
 
 
 def solution(mesh):
@@ -507,4 +542,4 @@
         P(),
         P(),
     )
-    return jax.shard_map(body, mesh=mesh, in_specs=in_specs, out_specs=P(("shot", "beam"), None, None), check_vma=False)
+    return jax.shard_map(functools.partial(body, mesh), mesh=mesh, in_specs=in_specs, out_specs=P(("shot", "beam"), None, None), check_vma=False)

time: 97.3 us -> 88.7 us (0.912)
  Pallas kernels: 93.9 us -> 86.8 us
  local copies, waits for them, and re-layouts: 3.1 us -> 1.67 us
    pallas_call x1, Pallas kernels: 91 us -> 84.8 us  [fused(): pl.pallas_call(functools.partial(kernel, mesh), out_shape=jax.ShapeDtypeS...]
    unnamed x2 -> x1, local copies, waits for them, and re-layouts: 3.1 us -> 1.67 us
    pallas_call x1, Pallas kernels: 2.98 us -> 1.97 us  [prep(): pl.pallas_call(prep_kernel, out_shape=jax.ShapeDtypeStruct((8, 128), jnp....]
where the time goes in v5:
time: 88.7 us; the launch traced here: 88.5 us
  Pallas kernels  86.8 us (98%)
  local copies, waits for them, and re-layouts  1.67 us (2%)
    pallas_call x1, Pallas kernels, fused(): pl.pallas_call(functools.partial(kernel, mesh), out_shape=jax.ShapeDtypeS...  84.8 us
    pallas_call x1, Pallas kernels, prep(): pl.pallas_call(prep_kernel, out_shape=jax.ShapeDtypeStruct((8, 128), jnp....  1.97 us

profile of v5, /device:TPU:1, one launch (start us, length us, event | category | flops | bytes accessed | tf_op | source)
XLA Modules:
  0.0 88.5 jit_solution(1468261081594551110)
XLA Ops:
  0.0 2.0 %entry_table.1.tab = s32[8,128]{1,0:T(8,128)} custom-call(s32[1,8]{1,0:T(1,128)} %count.1, s32[8,12]{1,0:T(8,128)} %index.1, s32[12,128]{1,0:T(8,128)} %bitcast.9, s32[12,128]{1,0:T(8,128)} %bitcast.10, s32[4,128]{1,0:T(4,128)} %bitcast.12), custom_call_target="tpu_custom_call" | custom-call | tf_op jit(solution)/shard_map/entry_table/pallas_call | solution.py:196
  2.0 84.8 %beam_migration.1 = f32[4,128,128]{2,1,0:T(8,128)} custom-call(s32[8,128]{1,0:T(8,128)} %entry_table.1.tab, bf16[256,128]{1,0:T(8,128)(2,1)} %bitcast.8, s32[16,16,16]{2,1,0:T(8,128)} %bitcast.7, s32[8,32]{1,0:T(8,128)} %bitcast.11, bf16[32,32,128]{2,1,0:T(8,128)(2,1)} %constant.4.clone.t0_hbm, bf16[32,32,128]{2,1,0:T(8,128)(2,1)} %constant.5.clone.t1_hbm, ...), custom_call_target="tpu_custom_call" | custom-call | tf_op jit(solution)/shard_map/beam_migration/pallas_call | solution.py:501
  86.8 1.7 %copy.14 = f32[4,128,128]{2,1,0:T(8,128)} copy(f32[4,128,128]{2,1,0:T(8,128)} %beam_migration.1) | data formatting | bytes 524288

commit v6 on v5

--- a/solution.py
+++ b/solution.py
@@ -80,20 +80,22 @@
         t = tdt[h, z, :]
         c1, s1 = sincos_turns((W0 + DW * MID) * t)
         uc, us = sincos_turns(DW * t)
-        seeds.append((c1 * uc + s1 * us, s1 * uc - c1 * us, c1, s1, uc + uc))
+        c0, s0 = c1 * uc + s1 * us, s1 * uc - c1 * us
+        seeds.append((c0 + s0, s0 - c0, c1 + s1, s1 - c1, uc + uc))
 
     def emit(f, st):
-        ar = ai = None
+        mid = re = im = None
         for h in range(2):
             br = bt[c, h, f : f + 1, :]
             bi = bt[c, h, NF + f : NF + f + 1, :]
-            cv, sv = st[h][2], st[h][3]
-            xr = br * cv - bi * sv
-            xi = br * sv + bi * cv
-            ar = xr if ar is None else ar + xr
-            ai = xi if ai is None else ai + xi
-        d_scr[f, 0, z, :] = ar.astype(BF16)
-        d_scr[f, 1, z, :] = ai.astype(BF16)
+            bm = bt[c, h, 2 * NF + f : 2 * NF + f + 1, :]
+            plus, minus = st[h][2], st[h][3]
+            k = (plus - minus) * bm
+            mid = k if mid is None else mid + k
+            re = bi * plus if re is None else re + bi * plus
+            im = br * minus if im is None else im + br * minus
+        d_scr[f, 0, z, :] = (mid - re).astype(BF16)
+        d_scr[f, 1, z, :] = (mid + im).astype(BF16)
 
     def step(st):
         return [(x[2], x[3], s[4] * x[2] - x[0], s[4] * x[3] - x[1]) for x, s in zip(st, seeds)]
@@ -393,10 +395,14 @@
             def _():
                 depth_send(e + 2)
 
+    def put_beams(c, h, v):
+        bt[c, h, 0 : 2 * NF] = v
+        bt[c, h, 2 * NF : 3 * NF] = 0.5 * (v[:NF] + v[NF:])
+
     def early(e):
         await_all(b_in.at[e, 0 : NS - 1], ber.at[e])
         for h in range(2):
-            bt[NC + e, h] = b_in[e, 4 * h : 4 * h + 4].reshape(128, 128).T
+            put_beams(NC + e, h, b_in[e, 4 * h : 4 * h + 4].reshape(128, 128).T)
 
     def pass_beams():
         for n in range(2):
@@ -414,7 +420,7 @@
 
         def turn(c, _):
             for h in range(2):
-                bt[c, h] = jnp.concatenate([ball[4 * h + s, c] for s in range(4)], 0).T
+                put_beams(c, h, jnp.concatenate([ball[4 * h + s, c] for s in range(4)], 0).T)
             return 0
 
         lax.fori_loop(0, NC, turn, 0)
@@ -509,7 +515,7 @@
             pltpu.VMEM((NG, 16, 128), BF16), pltpu.VMEM((NG, 16, 128), BF16),
             pltpu.VMEM((NC, WIN, 128), F32), pltpu.VMEM((NC, WIN, 128), F32),
             pltpu.VMEM((NS, NC, NP, 128), F32), pltpu.VMEM((NC, NP, 128), F32), pltpu.VMEM((NS, EARLY, NP, 128), F32), pltpu.VMEM((EARLY, NS, NP, 128), F32),
-            pltpu.VMEM((NC + EARLY, 2, 128, 128), F32),
+            pltpu.VMEM((NC + EARLY, 2, 192, 128), F32),
             pltpu.VMEM((NS, NE, NP, 128), F32), pltpu.VMEM((NE, NS, NP, 128), F32), pltpu.VMEM((2, 128, 128), F32),
             pltpu.VMEM((NF, 2, 128, 128), BF16), pltpu.VMEM((NF, 2, 128, 128), BF16),
             pltpu.VMEM((NE, 2, NF, NP, 128), BF16),

time: 88.7 us -> 88 us (level)
  no operation moved by 1% of the time
where the time goes in v6:
time: 88 us; the launch traced here: 87.8 us
  Pallas kernels  86.1 us (98%)
  local copies, waits for them, and re-layouts  1.67 us (2%)
    pallas_call x1, Pallas kernels, fused(): pl.pallas_call(functools.partial(kernel, mesh), out_shape=jax.ShapeDtypeS...  84.1 us
    pallas_call x1, Pallas kernels, prep(): pl.pallas_call(prep_kernel, out_shape=jax.ShapeDtypeStruct((8, 128), jnp....  1.97 us

profile of v6, /device:TPU:1, one launch (start us, length us, event | category | flops | bytes accessed | tf_op | source)
XLA Modules:
  0.0 87.8 jit_solution(3732223895867047233)
XLA Ops:
  0.0 2.0 %entry_table.1.tab = s32[8,128]{1,0:T(8,128)} custom-call(s32[1,8]{1,0:T(1,128)} %count.1, s32[8,12]{1,0:T(8,128)} %index.1, s32[12,128]{1,0:T(8,128)} %bitcast.9, s32[12,128]{1,0:T(8,128)} %bitcast.10, s32[4,128]{1,0:T(4,128)} %bitcast.12), custom_call_target="tpu_custom_call" | custom-call | tf_op jit(solution)/shard_map/entry_table/pallas_call | solution.py:198
  2.0 84.1 %beam_migration.1 = f32[4,128,128]{2,1,0:T(8,128)} custom-call(s32[8,128]{1,0:T(8,128)} %entry_table.1.tab, bf16[256,128]{1,0:T(8,128)(2,1)} %bitcast.8, s32[16,16,16]{2,1,0:T(8,128)} %bitcast.7, s32[8,32]{1,0:T(8,128)} %bitcast.11, bf16[32,32,128]{2,1,0:T(8,128)(2,1)} %constant.4.clone.t0_hbm, bf16[32,32,128]{2,1,0:T(8,128)(2,1)} %constant.5.clone.t1_hbm, ...), custom_call_target="tpu_custom_call" | custom-call | tf_op jit(solution)/shard_map/beam_migration/pallas_call | solution.py:507
  86.1 1.7 %copy.14 = f32[4,128,128]{2,1,0:T(8,128)} copy(f32[4,128,128]{2,1,0:T(8,128)} %beam_migration.1) | data formatting | bytes 524288

commit v7 on v6

--- a/solution.py
+++ b/solution.py
@@ -362,6 +362,7 @@
     depth_send(1)
     for e in range(1, EARLY):
         early_send(e)
+    depth_send(2)
     ball[shot] = b_own[...]
     lax.fori_loop(NE // 2, NE, lat, 0)
 
@@ -387,13 +388,13 @@
         if after is not None:
             after()
         if isinstance(e, int):
-            depth_send(e + 2)
+            depth_send(e + 3)
         else:
             relay(e - 2)
 
-            @pl.when(e + 2 < NE)
+            @pl.when(e + 3 < NE)
             def _():
-                depth_send(e + 2)
+                depth_send(e + 3)
 
     def put_beams(c, h, v):
         bt[c, h, 0 : 2 * NF] = v

time: 88 us -> 83.1 us (0.944)
  Pallas kernels: 86.1 us -> 81.2 us
    pallas_call x1, Pallas kernels: 84.1 us -> 79.2 us  [fused(): pl.pallas_call(functools.partial(kernel, mesh), out_shape=jax.ShapeDtypeS...]
where the time goes in v7:
time: 83.1 us; the launch traced here: 82.9 us
  Pallas kernels  81.2 us (98%)
  local copies, waits for them, and re-layouts  1.67 us (2%)
    pallas_call x1, Pallas kernels, fused(): pl.pallas_call(functools.partial(kernel, mesh), out_shape=jax.ShapeDtypeS...  79.2 us
    pallas_call x1, Pallas kernels, prep(): pl.pallas_call(prep_kernel, out_shape=jax.ShapeDtypeStruct((8, 128), jnp....  1.97 us
    unnamed x1, local copies, waits for them, and re-layouts  1.67 us

profile of v7, /device:TPU:1, one launch (start us, length us, event | category | flops | bytes accessed | tf_op | source)
XLA Modules:
  0.0 82.9 jit_solution(13096261603122544943)
XLA Ops:
  0.0 2.0 %entry_table.1.tab = s32[8,128]{1,0:T(8,128)} custom-call(s32[1,8]{1,0:T(1,128)} %count.1, s32[8,12]{1,0:T(8,128)} %index.1, s32[12,128]{1,0:T(8,128)} %bitcast.9, s32[12,128]{1,0:T(8,128)} %bitcast.10, s32[4,128]{1,0:T(4,128)} %bitcast.12), custom_call_target="tpu_custom_call" | custom-call | tf_op jit(solution)/shard_map/entry_table/pallas_call | solution.py:198
  2.0 79.2 %beam_migration.1 = f32[4,128,128]{2,1,0:T(8,128)} custom-call(s32[8,128]{1,0:T(8,128)} %entry_table.1.tab, bf16[256,128]{1,0:T(8,128)(2,1)} %bitcast.8, s32[16,16,16]{2,1,0:T(8,128)} %bitcast.7, s32[8,32]{1,0:T(8,128)} %bitcast.11, bf16[32,32,128]{2,1,0:T(8,128)(2,1)} %constant.4.clone.t0_hbm, bf16[32,32,128]{2,1,0:T(8,128)(2,1)} %constant.5.clone.t1_hbm, ...), custom_call_target="tpu_custom_call" | custom-call | tf_op jit(solution)/shard_map/beam_migration/pallas_call | solution.py:508
  81.2 1.7 %copy.14 = f32[4,128,128]{2,1,0:T(8,128)} copy(f32[4,128,128]{2,1,0:T(8,128)} %beam_migration.1) | data formatting | bytes 524288
